TPU v7x, 256 devices: a whole 4x4x8 slice. The times are simulated.
256 devices in a mesh: occ: 16 (over z_hi, y), fit: 16 (over x, z_lo, core).
Axes of the slice: x: 4, y: 4, z: 8 (z_hi: 4, z_lo: 2; z = z_hi * 2 + z_lo), core: 2. Of those that a mesh axis runs over, the one named last changes fastest.
Arguments:
- integrals: bfloat16 [8192, 16, 512], P('fit', 'occ'), may hold values from -0.62890625 to 0.62890625
- fitting: bfloat16 [8192, 8192], P('fit', 'occ'), may hold values from -0.1 to 1.1
- occ_energy: float32 [16], P('occ'), may hold values from -2 to -0.5
- vir_energy: float32 [512], replicated, may hold values from 0.2 to 3
Outputs:
- density: float32 [8192, 16, 512], P('fit', 'occ')
- pair_energy: float32 [16, 6], P('occ')
All inputs are finite; a program needn't handle non-finite values.
Results may differ from a plain program's by a relative error of at most 0.0003.
Values may be sent and summed in bfloat16 or wider, within the bound.
A program may use at most 64 MiB of HBM per device.

v0:
```python
import jax
import jax.numpy as jnp
from jax import lax
from jax.sharding import PartitionSpec as P

STOPS = 6


def passed_along(block, axis, distance):
    devices = range(lax.axis_size(axis))
    route = [((i - distance) % len(devices), i) for i in devices]
    return lax.ppermute(block, axis, route)


def body(integrals, fitting, occ_energy, vir_energy):
    metric = lax.all_gather(fitting, "occ", axis=1, tiled=True)
    nvir = integrals.shape[2]
    fitted = jnp.dot(
        metric,
        lax.all_gather(integrals, "fit", axis=0, tiled=True)[:, 0, :],
        preferred_element_type=jnp.float32,
    )
    own_energy = occ_energy[0]
    partner = fitted
    partner_energy = occ_energy
    density = jnp.zeros_like(fitted)
    energies = []
    for step in range(STOPS):
        if step > 0:
            partner, partner_energy = passed_along((partner, partner_energy), "occ", -1)
        local_pair = lax.dot_general(
            fitted,
            partner,
            (((0,), (0,)), ((), ())),
            precision=lax.Precision.HIGHEST,
            preferred_element_type=jnp.float32,
        )
        denom = own_energy + partner_energy[0] - vir_energy[:, None] - vir_energy[None, :]
        summed = lax.psum(local_pair, "fit")
        amplitude = summed / denom
        energies.append(jnp.sum(amplitude * (2.0 * summed - summed.T)) / (nvir * nvir))
        density = density + jnp.dot(
            partner,
            amplitude.T,
            precision=lax.Precision.HIGHEST,
            preferred_element_type=jnp.float32,
        )
    pair_energy = jnp.stack(energies)[None, :]
    return (density[:, None, :], pair_energy)


def solution(mesh):
    placed = (P("fit", "occ", None), P("fit", "occ"), P("occ"), P())
    return jax.shard_map(
        body,
        mesh=mesh,
        in_specs=placed,
        out_specs=(P("fit", "occ", None), P("occ", None)),
        check_vma=False,
    )
```

profile of v0, /device:TPU:1, one launch (start us, length us, event | category | flops | bytes accessed | tf_op | source)
XLA Modules:
  0.0 690.5 jit_solution(18398459056344166789)
XLA Ops:
  8.7 129.6 %all-gather.3.cloned.1.call-done = bf16[512,8192]{1,0:T(8,128)(2,1)} async-done(((bf16[512,512]{1,0:T(8,128)(2,1)}), bf16[512,8192]{1,0:T(8,128)(2,1)}) %all-gather.3.cloned.1.call-update) | async-done | bytes 8388624 | tf_op jit(solution)/shard_map/all_gather | solution.py:16
  138.3 54.8 %all-gather.5.cloned.1.call-done = bf16[8192,1,512]{2,0,1:T(8,128)(2,1)} async-done(((bf16[512,1,512]{2,0,1:T(8,128)(2,1)}), bf16[8192,1,512]{2,0,1:T(8,128)(2,1)}) %all-gather.5.cloned.1.call-update) | async-done | bytes 8388624 | tf_op jit(solution)/shard_map/all_gather | solution.py:20
  193.1 9.4 %fusion = f32[512,512]{1,0:T(8,128)S(1)} fusion(bf16[512,8192]{1,0:T(8,128)(2,1)} %all-gather.3.cloned.1.call-done, bf16[8192,1,512]{2,0,1:T(8,128)(2,1)} %all-gather.5.cloned.1.call-done), kind=kOutput, calls=%fused_computation | convolution fusion | flops 4294967296 | bytes 17825792 | tf_op jit(solution)/shard_map/dot_general | solution.py:18
  202.5 5.9 collective-permute-start
  208.5 54.2 %collective-permute-done = f32[512,512]{1,0:T(8,128)S(1)} collective-permute-done((f32[512,512]{1,0:T(8,128)S(1)}, f32[512,512]{1,0:T(8,128)S(1)}, u32[]{:S(2)}, u32[]{:S(2)}) %collective-permute-start) | collective-permute-done | bytes 1048608 | tf_op jit(solution)/shard_map/ppermute | solution.py:12
  262.7 22.3 %collective-permute-start.2 = (f32[512,512]{1,0:T(8,128)S(1)}, f32[512,512]{1,0:T(8,128)S(1)}, u32[]{:S(2)}, u32[]{:S(2)}) collective-permute-start(f32[512,512]{1,0:T(8,128)S(1)} %collective-permute-done), channel_id=1, source_target_pairs={{16,0},{32,16},{48,32},{64,48},{80,64},{96,80},{112,96},{128,112},... | collective-permute-start | bytes 3145736 | tf_op jit(solution)/shard_map/ppermute | solution.py:12
  285.0 47.6 %collective-permute-done.2 = f32[512,512]{1,0:T(8,128)S(1)} collective-permute-done((f32[512,512]{1,0:T(8,128)S(1)}, f32[512,512]{1,0:T(8,128)S(1)}, u32[]{:S(2)}, u32[]{:S(2)}) %collective-permute-start.2) | collective-permute-done | bytes 1048608 | tf_op jit(solution)/shard_map/ppermute | solution.py:12
  332.6 6.4 collective-permute-start.4
  339.0 47.4 %collective-permute-done.4 = f32[512,512]{1,0:T(8,128)S(1)} collective-permute-done((f32[512,512]{1,0:T(8,128)S(1)}, f32[512,512]{1,0:T(8,128)S(1)}, u32[]{:S(2)}, u32[]{:S(2)}) %collective-permute-start.4) | collective-permute-done | bytes 1048608 | tf_op jit(solution)/shard_map/ppermute | solution.py:12
  386.4 6.4 collective-permute-start.6
  395.7 32.2 %collective-permute-done.6 = f32[512,512]{1,0:T(8,128)S(1)} collective-permute-done((f32[512,512]{1,0:T(8,128)S(1)}, f32[512,512]{1,0:T(8,128)S(1)}, u32[]{:S(2)}, u32[]{:S(2)}) %collective-permute-start.6) | collective-permute-done | bytes 1048608 | tf_op jit(solution)/shard_map/ppermute | solution.py:12
  427.9 6.7 collective-permute-start.8
  445.9 10.6 %collective-permute-done.8 = f32[512,512]{1,0:T(8,128)S(1)} collective-permute-done((f32[512,512]{1,0:T(8,128)S(1)}, f32[512,512]{1,0:T(8,128)S(1)}, u32[]{:S(2)}, u32[]{:S(2)}) %collective-permute-start.8) | collective-permute-done | bytes 1048608 | tf_op jit(solution)/shard_map/ppermute | solution.py:12
  460.4 6.5 collective-permute-start.1
  467.8 6.0 collective-permute-start.3
  474.8 6.0 collective-permute-start.5
  481.7 5.9 collective-permute-start.7
  488.4 5.9 collective-permute-start.9
  495.7 123.2 %all-reduce.3.cloned.1.call-done = (f32[512,512]{1,0:T(8,128)}, f32[512,512]{1,0:T(8,128)}, f32[512,512]{1,0:T(8,128)}, f32[512,512]{1,0:T(8,128)}, f32[512,512]{1,0:T(8,128)}, /*index=5*/f32[512,512]{1,0:T(8,128)}) async-done(((f32[512,512]{1,0:T(8,128)}, f32[512,512]{1,0:T(8,128)}, f32[512,512]{1,0:T(8,128)}, f32[512,512]{1,0:T(8,128)}, f32[512,512]{1,0:T(8,128)}, /*index=5*/f32[512,512]{1,0:T(8,128)}), ...) | async-done | bytes 6291472 | tf_op jit(solution)/shard_map/psum | solution.py:39
  635.0 13.8 %multiply_reduce_fusion = (f32[]{:T(128)}, f32[]{:T(128)}, f32[]{:T(128)}, f32[]{:T(128)}) fusion(f32[512,512]{1,0:T(8,128)} %copy.16, f32[512,512]{1,0:T(8,128)} %get-tuple-element.14, f32[512]{0:T(512)S(1)} %copy-done.13, f32[512]{0:T(512)S(1)} %get-tuple-element.21, f32[512,512]{1,0:T(8,128)} %copy.13, f32[512,512]{1,0:T(8,128)} %get-tuple-element.11, ...), kind=kLoop, calls=%fused_computation.14 | loop fusion | flops 6291452 | bytes 8398864 | tf_op jit(solution)/shard_map/reduce_sum | solution.py:41
  656.4 4.3 fusion.15
  665.5 4.0 convolution_add_fusion.4
  669.6 3.7 convolution_add_fusion.3
  673.3 3.6 convolution_add_fusion.2
  (60 shorter events, 51.9 us)
Async XLA Ops:
  7.2 131.1 %all-gather.3.cloned.1.call-start = ((), (), s32[]{:S(2)}) async-start(), calls=%async_computation | async-start | bytes 8912896 | tf_op jit(solution)/shard_map/all_gather | solution.py:16
  7.9 185.2 %all-gather.5.cloned.1.call-start = ((), (), s32[]{:S(2)}) async-start(), calls=%async_computation.1 | async-start | bytes 8912896 | tf_op jit(solution)/shard_map/all_gather | solution.py:20
  8.6 610.2 %all-reduce.3.cloned.1.call-start = ((), (), s32[]{:S(2)}) async-start(), calls=%async_computation.2 | async-start | bytes 12582912 | tf_op jit(solution)/shard_map/psum | solution.py:39
  202.5 60.2 %collective-permute-start = (f32[512,512]{1,0:T(8,128)S(1)}, f32[512,512]{1,0:T(8,128)S(1)}, u32[]{:S(2)}, u32[]{:S(2)}) collective-permute-start(f32[512,512]{1,0:T(8,128)S(1)} %fusion), channel_id=1, source_target_pairs={{16,0},{32,16},{48,32},{64,48},{80,64},{96,80},{112,96},{128,112},... | collective-permute-start | bytes 3145736 | tf_op jit(solution)/shard_map/ppermute | solution.py:12
  262.7 171.9 %copy-start.6 = (f32[512,512]{1,0:T(8,128)}, f32[512,512]{1,0:T(8,128)S(1)}, u32[]{:S(2)}) copy-start(f32[512,512]{1,0:T(8,128)S(1)} %collective-permute-done) | copy-start | bytes 3145732
  262.7 69.9 %collective-permute-start.2 = (f32[512,512]{1,0:T(8,128)S(1)}, f32[512,512]{1,0:T(8,128)S(1)}, u32[]{:S(2)}, u32[]{:S(2)}) collective-permute-start(f32[512,512]{1,0:T(8,128)S(1)} %collective-permute-done), channel_id=1, source_target_pairs={{16,0},{32,16},{48,32},{64,48},{80,64},{96,80},{112,96},{128,112},... | collective-permute-start | bytes 3145736 | tf_op jit(solution)/shard_map/ppermute | solution.py:12
  332.6 104.8 %copy-start.7 = (f32[512,512]{1,0:T(8,128)}, f32[512,512]{1,0:T(8,128)S(1)}, u32[]{:S(2)}) copy-start(f32[512,512]{1,0:T(8,128)S(1)} %collective-permute-done.2) | copy-start | bytes 3145732
  332.6 53.8 %collective-permute-start.4 = (f32[512,512]{1,0:T(8,128)S(1)}, f32[512,512]{1,0:T(8,128)S(1)}, u32[]{:S(2)}, u32[]{:S(2)}) collective-permute-start(f32[512,512]{1,0:T(8,128)S(1)} %collective-permute-done.2), channel_id=1, source_target_pairs={{16,0},{32,16},{48,32},{64,48},{80,64},{96,80},{112,96},{128,112},... | collective-permute-start | bytes 3145736 | tf_op jit(solution)/shard_map/ppermute | solution.py:12
  386.4 53.9 %copy-start.8 = (f32[512,512]{1,0:T(8,128)}, f32[512,512]{1,0:T(8,128)S(1)}, u32[]{:S(2)}) copy-start(f32[512,512]{1,0:T(8,128)S(1)} %collective-permute-done.4) | copy-start | bytes 3145732
  386.4 41.5 %collective-permute-start.6 = (f32[512,512]{1,0:T(8,128)S(1)}, f32[512,512]{1,0:T(8,128)S(1)}, u32[]{:S(2)}, u32[]{:S(2)}) collective-permute-start(f32[512,512]{1,0:T(8,128)S(1)} %collective-permute-done.4), channel_id=1, source_target_pairs={{16,0},{32,16},{48,32},{64,48},{80,64},{96,80},{112,96},{128,112},... | collective-permute-start | bytes 3145736 | tf_op jit(solution)/shard_map/ppermute | solution.py:12
  427.9 15.2 %copy-start.9 = (f32[512,512]{1,0:T(8,128)}, f32[512,512]{1,0:T(8,128)S(1)}, u32[]{:S(2)}) copy-start(f32[512,512]{1,0:T(8,128)S(1)} %collective-permute-done.6) | copy-start | bytes 3145732
  427.9 28.7 %collective-permute-start.8 = (f32[512,512]{1,0:T(8,128)S(1)}, f32[512,512]{1,0:T(8,128)S(1)}, u32[]{:S(2)}, u32[]{:S(2)}) collective-permute-start(f32[512,512]{1,0:T(8,128)S(1)} %collective-permute-done.6), channel_id=1, source_target_pairs={{16,0},{32,16},{48,32},{64,48},{80,64},{96,80},{112,96},{128,112},... | collective-permute-start | bytes 3145736 | tf_op jit(solution)/shard_map/ppermute | solution.py:12
  440.3 55.4 %copy-start.13 = (f32[512]{0:T(512)S(1)}, f32[512]{0:T(512)}, u32[]{:S(2)}) copy-start(f32[512]{0:T(512)} %param.7) | copy-start | bytes 6148
  460.4 7.4 %collective-permute-start.1 = (f32[1]{0:T(128)}, f32[1]{0:T(128)}, u32[]{:S(2)}, u32[]{:S(2)}) collective-permute-start(f32[1]{0:T(128)} %param.6), channel_id=1, source_target_pairs={{16,0},{32,16},{48,32},{64,48},{80,64},{96,80},{112,96},{128,112},... | collective-permute-start | bytes 20 | tf_op jit(solution)/shard_map/ppermute | solution.py:12
  467.8 7.0 %collective-permute-start.3 = (f32[1]{0:T(128)}, f32[1]{0:T(128)}, u32[]{:S(2)}, u32[]{:S(2)}) collective-permute-start(f32[1]{0:T(128)} %collective-permute-done.1), channel_id=1, source_target_pairs={{16,0},{32,16},{48,32},{64,48},{80,64},{96,80},{112,96},{128,112},... | collective-permute-start | bytes 20 | tf_op jit(solution)/shard_map/ppermute | solution.py:12
  474.8 7.0 %collective-permute-start.5 = (f32[1]{0:T(128)}, f32[1]{0:T(128)}, u32[]{:S(2)}, u32[]{:S(2)}) collective-permute-start(f32[1]{0:T(128)} %collective-permute-done.3), channel_id=1, source_target_pairs={{16,0},{32,16},{48,32},{64,48},{80,64},{96,80},{112,96},{128,112},... | collective-permute-start | bytes 20 | tf_op jit(solution)/shard_map/ppermute | solution.py:12
  481.7 6.6 collective-permute-start.7
  488.4 6.7 collective-permute-start.9
  618.9 13.4 %copy-start.4 = (f32[512,512]{1,0:T(8,128)S(1)}, f32[512,512]{1,0:T(8,128)}, u32[]{:S(2)}) copy-start(f32[512,512]{1,0:T(8,128)} %get-tuple-element.13) | copy-start | bytes 3145732
  618.9 14.8 %copy-start.2 = (f32[512,512]{1,0:T(8,128)S(1)}, f32[512,512]{1,0:T(8,128)}, u32[]{:S(2)}) copy-start(f32[512,512]{1,0:T(8,128)} %get-tuple-element.14) | copy-start | bytes 3145732
  635.0 25.7 %copy-start = (f32[512,512]{1,0:T(8,128)S(1)}, f32[512,512]{1,0:T(8,128)}, u32[]{:S(2)}) copy-start(f32[512,512]{1,0:T(8,128)} %get-tuple-element.10) | copy-start | bytes 3145732
  635.0 25.7 %copy-start.1 = (f32[512,512]{1,0:T(8,128)S(1)}, f32[512,512]{1,0:T(8,128)}, u32[]{:S(2)}) copy-start(f32[512,512]{1,0:T(8,128)} %get-tuple-element.15) | copy-start | bytes 3145732
  665.5 13.5 %copy-start.5 = (f32[512,512]{0,1:T(8,128)S(1)}, f32[512,512]{0,1:T(8,128)}, u32[]{:S(2)}) copy-start(f32[512,512]{0,1:T(8,128)} %copy.11) | copy-start | bytes 3145732
  665.5 13.5 %copy-start.12 = (f32[512,512]{1,0:T(8,128)S(1)}, f32[512,512]{1,0:T(8,128)}, u32[]{:S(2)}) copy-start(f32[512,512]{1,0:T(8,128)} %copy-done.11) | copy-start | bytes 3145732
  (3 other events, 26.4 us)
Sparse Core Ops, SparseCore 0:
  10.4 127.8 all-gather.2
  140.2 52.8 all-gather.4
  460.6 158.2 all-reduce.2
where the time goes:
time: 699 us; the launch traced here: 690 us
  waiting for transfers between devices  502 us (72%)
  starting transfers between devices  78.1 us (11%)
  matrix products  46.2 us (7%)
  between operations  22.1 us (3%)
  local copies, waits for them, and re-layouts  21.8 us (3%)
  other arithmetic  20.3 us (3%)
    ppermute x10, waiting for transfers between devices, passed_along(): return lax.ppermute(block, axis, route)  193 us
    all_gather x1, waiting for transfers between devices, body(): metric = lax.all_gather(fitting, 'occ', axis=1, tiled=True)  130 us
    psum x1, waiting for transfers between devices, body(): summed = lax.psum(local_pair, 'fit')  123 us
    ppermute x10, starting transfers between devices, passed_along(): return lax.ppermute(block, axis, route)  78 us
    all_gather x1, waiting for transfers between devices, body(): lax.all_gather(integrals, 'fit', axis=0, tiled=True)[:, 0, :]  54.8 us
    dot_general x6, matrix products, body(): jnp.dot(partner, amplitude.T, precision=lax.Precision.HIGHEST, preferred_...  19.7 us
    reduce_sum x2, other arithmetic, body(): jnp.sum(amplitude * (2.0 * summed - summed.T)) / (nvir * nvir)  17.2 us
    dot_general x6, matrix products, body(): lax.dot_general(fitted, partner, (((0,), (0,)), ((), ())), precision=lax....  17.1 us
  transfers between devices with their start and end apart: 13, of which 13 were waited for; matrix products, arithmetic and copies ran while one was open for 2% of the time, Pallas kernels for 0%

commit v1 on v0

--- a/solution.py
+++ b/solution.py
@@ -1,9 +1,200 @@
+import functools
+
 import jax
 import jax.numpy as jnp
 from jax import lax
+from jax.experimental import pallas as pl
+from jax.experimental.pallas import tpu as pltpu
 from jax.sharding import PartitionSpec as P
 
 STOPS = 6
+MESH = pl.DeviceIdType.MESH
+HALVES = (pl.ds(0, 256), pl.ds(256, 256))
+
+
+class Place:
+    def __init__(self):
+        self.occ = lax.axis_index("occ")
+        self.fit = lax.axis_index("fit")
+        self.z, self.y = self.occ // 4, self.occ % 4
+        self.x, self.low, self.core = self.fit // 4, (self.fit // 2) % 2, self.fit % 2
+
+    def o(self, dz, dy):
+        return ((self.z + dz + 4) % 4) * 4 + (self.y + dy + 4) % 4
+
+    def f(self, dx, flip_low=0, flip_core=0):
+        low = self.low if not flip_low else 1 - self.low
+        core = self.core if not flip_core else 1 - self.core
+        return ((self.x + dx + 4) % 4) * 4 + low * 2 + core
+
+
+def entry_barrier(peers):
+    barrier = pltpu.get_barrier_semaphore()
+    for occ, fit in peers:
+        pl.semaphore_signal(barrier, inc=1, device_id={"occ": occ, "fit": fit}, device_id_type=MESH)
+    pl.semaphore_wait(barrier, len(peers))
+
+
+def fit_kernel(fit_ref, int_ref, out_ref, fb, ib, fsend, frecv, isend, irecv):
+    at = Place()
+    me = (at.occ, at.fit)
+    entry_barrier(
+        [(at.o(dz, dy), at.fit) for dz, dy in ((1, 0), (-1, 0), (0, 1), (0, -1))]
+        + [(at.occ, at.f(1)), (at.occ, at.f(-1)), (at.occ, at.f(0, 1)), (at.occ, at.f(0, 0, 1))]
+    )
+    started = []
+
+    def send(buf, recv, sends, src, slot, half, occ, fit):
+        at_half = () if half is None else (HALVES[half],)
+        sem = sends.at[len(started)]
+        copy = pltpu.make_async_remote_copy(
+            src_ref=src.at[at_half] if half is not None else src,
+            dst_ref=buf.at[(slot,) + at_half],
+            send_sem=sem,
+            recv_sem=recv.at[slot, 0 if half is None else half],
+            device_id={"occ": occ, "fit": fit},
+            device_id_type=MESH,
+        )
+        copy.start()
+        started.append(copy)
+
+    def arrived(buf, recv, slot, half):
+        part = buf.at[slot] if half is None else buf.at[slot, HALVES[half]]
+        pltpu.make_async_remote_copy(
+            src_ref=part,
+            dst_ref=part,
+            send_sem=fsend.at[0],
+            recv_sem=recv.at[slot, 0 if half is None else half],
+            device_id={"occ": me[0], "fit": me[1]},
+            device_id_type=MESH,
+        ).wait_recv()
+
+    def fsnd(src, slot, half, dz, dy):
+        send(fb, frecv, fsend, src, slot, half, at.o(dz, dy), at.fit)
+
+    def isnd(src, slot, half, fit):
+        send(ib, irecv, fsend, src, slot, half, at.occ, fit)
+
+    def f_got(dz, dy):
+        slot = at.o(dz, dy)
+        if dz == 2 and dy == 0 or dy == 2:
+            arrived(fb, frecv, slot, 0)
+            arrived(fb, frecv, slot, 1)
+        else:
+            arrived(fb, frecv, slot, None)
+        return slot
+
+    def i_got(dx, flip_low):
+        slot = at.f(dx, flip_low)
+        if dx == 2:
+            arrived(ib, irecv, slot, 0)
+            arrived(ib, irecv, slot, 1)
+        else:
+            arrived(ib, irecv, slot, None)
+        return slot
+
+    def f_spread(dz):
+        slot = at.o(dz, 0)
+        src = fit_ref if dz == 0 else fb.at[slot]
+        fsnd(src, slot, None, 0, 1)
+        fsnd(src, slot, None, 0, -1)
+
+    def f_relay_y(dz):
+        slot = f_got(dz, 1)
+        fsnd(fb.at[slot], slot, 0, 0, -1)
+        slot = f_got(dz, -1)
+        fsnd(fb.at[slot], slot, 1, 0, 1)
+
+    def to_core(src, slot):
+        isnd(src, slot, None, at.f(0, 0, 1))
+
+    def i_spread(flip_low):
+        slot = at.f(0, flip_low)
+        src = ib.at[slot] if flip_low else int_ref
+        isnd(src, slot, None, at.f(1))
+        isnd(src, slot, None, at.f(-1))
+
+    def i_relay(flip_low):
+        slot = i_got(1, flip_low)
+        isnd(ib.at[slot], slot, 0, at.f(-1))
+        to_core(ib.at[slot], slot)
+        slot = i_got(-1, flip_low)
+        isnd(ib.at[slot], slot, 1, at.f(1))
+        to_core(ib.at[slot], slot)
+
+    def multiply(dy):
+        for dz in (0, 1, -1, 2):
+            if dy == 2:
+                f_got(dz, 2)
+
+        def one(k, carry):
+            slot = at.o(k, dy)
+            out_ref[...] += jnp.dot(fb[slot], ib[slot], preferred_element_type=jnp.float32)
+            return carry
+
+        lax.fori_loop(0, 4, one, 0)
+
+    fsnd(fit_ref, at.occ, None, 1, 0)
+    fsnd(fit_ref, at.occ, None, -1, 0)
+    f_spread(0)
+    i_spread(0)
+    to_core(int_ref, at.fit)
+    fb[at.occ] = fit_ref[...]
+    ib[at.fit] = int_ref[...]
+    out_ref[...] = jnp.zeros_like(out_ref)
+
+    f_relay_y(0)
+    i_relay(0)
+    slot = i_got(2, 0)
+    to_core(ib.at[slot], slot)
+    slot = f_got(1, 0)
+    fsnd(fb.at[slot], slot, 0, -1, 0)
+    f_spread(1)
+    slot = f_got(-1, 0)
+    fsnd(fb.at[slot], slot, 1, 1, 0)
+    f_spread(-1)
+    isnd(int_ref, at.fit, None, at.f(0, 1))
+    f_got(2, 0)
+    f_spread(2)
+    slot = i_got(0, 1)
+    i_spread(1)
+    to_core(ib.at[slot], slot)
+    f_relay_y(1)
+    i_relay(1)
+    f_relay_y(-1)
+    slot = i_got(2, 1)
+    to_core(ib.at[slot], slot)
+    f_relay_y(2)
+    for flip_low in (0, 1):
+        for dx in (0, 1, -1, 2):
+            arrived(ib, irecv, at.f(dx, flip_low, 1), None)
+    multiply(0)
+    multiply(1)
+    multiply(3)
+    multiply(2)
+    for copy in started:
+        copy.wait_send()
+
+
+def fitted_of(fitting, integrals):
+    sends = 37
+    return pl.pallas_call(
+        fit_kernel,
+        out_shape=jax.ShapeDtypeStruct((512, 512), jnp.float32),
+        in_specs=[pl.BlockSpec(memory_space=pltpu.VMEM)] * 2,
+        out_specs=pl.BlockSpec(memory_space=pltpu.VMEM),
+        scratch_shapes=[
+            pltpu.VMEM((16, 512, 512), jnp.bfloat16),
+            pltpu.VMEM((16, 512, 512), jnp.bfloat16),
+            pltpu.SemaphoreType.DMA((sends,)),
+            pltpu.SemaphoreType.DMA((16, 2)),
+            pltpu.SemaphoreType.DMA((1,)),
+            pltpu.SemaphoreType.DMA((16, 2)),
+        ],
+        compiler_params=pltpu.CompilerParams(
+            collective_id=0, has_side_effects=True, vmem_limit_bytes=40 * 1024 * 1024
+        ),
+    )(fitting, integrals)
 
 
 def passed_along(block, axis, distance):
@@ -13,13 +204,8 @@
 
 
 def body(integrals, fitting, occ_energy, vir_energy):
-    metric = lax.all_gather(fitting, "occ", axis=1, tiled=True)
     nvir = integrals.shape[2]
-    fitted = jnp.dot(
-        metric,
-        lax.all_gather(integrals, "fit", axis=0, tiled=True)[:, 0, :],
-        preferred_element_type=jnp.float32,
-    )
+    fitted = fitted_of(fitting, integrals[:, 0, :])
     own_energy = occ_energy[0]
     partner = fitted
     partner_energy = occ_energy

time: 699 us -> 573 us (0.82)
  waiting for transfers between devices: 502 us -> 320 us
  Pallas kernels: 0 us -> 87.3 us
  starting transfers between devices: 78.1 us -> 59.4 us
  matrix products: 46.2 us -> 33.8 us
    all_gather x2 -> x0, waiting for transfers between devices: 184 us -> none  [the longest x1 130 us: body(): metric = lax.all_gather(fitting, 'occ', axis=1, tiled=True)]
    pallas_call x0 -> x1, Pallas kernels: none -> 87.3 us  [fitted_of(): pl.pallas_call(fit_kernel, out_shape=jax.ShapeDtypeStruct((512, 512), jnp...]
    ppermute x10, starting transfers between devices: 78 us -> 59.3 us  [passed_along(): return lax.ppermute(block, axis, route)]
    dot_general x1 -> x0, matrix products: 9.44 us -> none  [body(): jnp.dot(metric, lax.all_gather(integrals, 'fit', axis=0, tiled=True)[:, 0...]
  transfers between devices with their start and end apart: 13 -> 11, of which waited for: 13 -> 11; matrix products, arithmetic and copies ran while one was open for 2% -> 3% of each run, Pallas kernels for 0% -> 0%
where the time goes in v1:
time: 573 us; the launch traced here: 565 us
  waiting for transfers between devices  320 us (56%)
  Pallas kernels  87.3 us (15%)
  starting transfers between devices  59.4 us (10%)
  matrix products  33.8 us (6%)
  local copies, waits for them, and re-layouts  25.9 us (5%)
  between operations  22.3 us (4%)
  other arithmetic  16.8 us (3%)
    ppermute x10, waiting for transfers between devices, passed_along(): return lax.ppermute(block, axis, route)  190 us
    psum x1, waiting for transfers between devices, body(): summed = lax.psum(local_pair, 'fit')  130 us
    pallas_call x1, Pallas kernels, fitted_of(): pl.pallas_call(fit_kernel, out_shape=jax.ShapeDtypeStruct((512, 512), jnp...  87.3 us
    ppermute x10, starting transfers between devices, passed_along(): return lax.ppermute(block, axis, route)  59.3 us
    dot_general x6, matrix products, body(): lax.dot_general(fitted, partner, (((0,), (0,)), ((), ())), precision=lax....  17.1 us
    dot_general x6, matrix products, body(): jnp.dot(partner, amplitude.T, precision=lax.Precision.HIGHEST, preferred_...  16.7 us
    reduce_sum x2, other arithmetic, body(): jnp.sum(amplitude * (2.0 * summed - summed.T)) / (nvir * nvir)  15.2 us
  transfers between devices with their start and end apart: 11, of which 11 were waited for; matrix products, arithmetic and copies ran while one was open for 3% of the time, Pallas kernels for 0%

profile of v1, /device:TPU:1, one launch (start us, length us, event | category | flops | bytes accessed | tf_op | source)
XLA Modules:
  0.0 565.5 jit_solution(8796631598112341262)
XLA Ops:
  9.3 87.3 %shard_map.59 = f32[512,512]{1,0:T(8,128)S(1)} custom-call(bf16[512,512]{1,0:T(8,128)(2,1)S(1)} %copy-done, bf16[512,512]{1,0:T(8,128)(2,1)S(1)} %bitcast.50), custom_call_target="tpu_custom_call" | custom-call | tf_op jit(solution)/shard_map/pallas_call | solution.py:181
  96.6 3.3 collective-permute-start
  99.9 45.1 %collective-permute-done = f32[512,512]{1,0:T(8,128)S(1)} collective-permute-done((f32[512,512]{1,0:T(8,128)S(1)}, f32[512,512]{1,0:T(8,128)S(1)}, u32[]{:S(2)}, u32[]{:S(2)}) %collective-permute-start) | collective-permute-done | bytes 1048608 | tf_op jit(solution)/shard_map/ppermute | solution.py:203
  145.0 6.4 %collective-permute-start.2 = (f32[512,512]{1,0:T(8,128)S(1)}, f32[512,512]{1,0:T(8,128)S(1)}, u32[]{:S(2)}, u32[]{:S(2)}) collective-permute-start(f32[512,512]{1,0:T(8,128)S(1)} %collective-permute-done), channel_id=1, source_target_pairs={{16,0},{32,16},{48,32},{64,48},{80,64},{96,80},{112,96},{128,112},... | collective-permute-start | bytes 3145736 | tf_op jit(solution)/shard_map/ppermute | solution.py:203
  151.4 31.2 %collective-permute-done.2 = f32[512,512]{1,0:T(8,128)S(1)} collective-permute-done((f32[512,512]{1,0:T(8,128)S(1)}, f32[512,512]{1,0:T(8,128)S(1)}, u32[]{:S(2)}, u32[]{:S(2)}) %collective-permute-start.2) | collective-permute-done | bytes 1048608 | tf_op jit(solution)/shard_map/ppermute | solution.py:203
  182.6 6.4 %collective-permute-start.4 = (f32[512,512]{1,0:T(8,128)S(1)}, f32[512,512]{1,0:T(8,128)S(1)}, u32[]{:S(2)}, u32[]{:S(2)}) collective-permute-start(f32[512,512]{1,0:T(8,128)S(1)} %collective-permute-done.2), channel_id=1, source_target_pairs={{16,0},{32,16},{48,32},{64,48},{80,64},{96,80},{112,96},{128,112},... | collective-permute-start | bytes 3145736 | tf_op jit(solution)/shard_map/ppermute | solution.py:203
  189.0 44.0 %collective-permute-done.4 = f32[512,512]{1,0:T(8,128)S(1)} collective-permute-done((f32[512,512]{1,0:T(8,128)S(1)}, f32[512,512]{1,0:T(8,128)S(1)}, u32[]{:S(2)}, u32[]{:S(2)}) %collective-permute-start.4) | collective-permute-done | bytes 1048608 | tf_op jit(solution)/shard_map/ppermute | solution.py:203
  233.0 6.4 %collective-permute-start.6 = (f32[512,512]{1,0:T(8,128)S(1)}, f32[512,512]{1,0:T(8,128)S(1)}, u32[]{:S(2)}, u32[]{:S(2)}) collective-permute-start(f32[512,512]{1,0:T(8,128)S(1)} %collective-permute-done.4), channel_id=1, source_target_pairs={{16,0},{32,16},{48,32},{64,48},{80,64},{96,80},{112,96},{128,112},... | collective-permute-start | bytes 3145736 | tf_op jit(solution)/shard_map/ppermute | solution.py:203
  242.3 43.0 %collective-permute-done.6 = f32[512,512]{1,0:T(8,128)S(1)} collective-permute-done((f32[512,512]{1,0:T(8,128)S(1)}, f32[512,512]{1,0:T(8,128)S(1)}, u32[]{:S(2)}, u32[]{:S(2)}) %collective-permute-start.6) | collective-permute-done | bytes 1048608 | tf_op jit(solution)/shard_map/ppermute | solution.py:203
  285.3 6.7 %collective-permute-start.8 = (f32[512,512]{1,0:T(8,128)S(1)}, f32[512,512]{1,0:T(8,128)S(1)}, u32[]{:S(2)}, u32[]{:S(2)}) collective-permute-start(f32[512,512]{1,0:T(8,128)S(1)} %collective-permute-done.6), channel_id=1, source_target_pairs={{16,0},{32,16},{48,32},{64,48},{80,64},{96,80},{112,96},{128,112},... | collective-permute-start | bytes 3145736 | tf_op jit(solution)/shard_map/ppermute | solution.py:203
  292.0 2.8 fusion.15
  294.8 2.9 fusion.16
  297.7 2.8 fusion.17
  300.5 2.9 fusion.18
  303.4 26.3 %collective-permute-done.8 = f32[512,512]{1,0:T(8,128)S(1)} collective-permute-done((f32[512,512]{1,0:T(8,128)S(1)}, f32[512,512]{1,0:T(8,128)S(1)}, u32[]{:S(2)}, u32[]{:S(2)}) %collective-permute-start.8) | collective-permute-done | bytes 1048608 | tf_op jit(solution)/shard_map/ppermute | solution.py:203
  333.5 6.5 %collective-permute-start.1 = (f32[1]{0:T(128)}, f32[1]{0:T(128)}, u32[]{:S(2)}, u32[]{:S(2)}) collective-permute-start(f32[1]{0:T(128)} %param.6), channel_id=1, source_target_pairs={{16,0},{32,16},{48,32},{64,48},{80,64},{96,80},{112,96},{128,112},... | collective-permute-start | bytes 20 | tf_op jit(solution)/shard_map/ppermute | solution.py:203
  340.9 5.9 %collective-permute-start.3 = (f32[1]{0:T(128)}, f32[1]{0:T(128)}, u32[]{:S(2)}, u32[]{:S(2)}) collective-permute-start(f32[1]{0:T(128)} %collective-permute-done.1), channel_id=1, source_target_pairs={{16,0},{32,16},{48,32},{64,48},{80,64},{96,80},{112,96},{128,112},... | collective-permute-start | bytes 20 | tf_op jit(solution)/shard_map/ppermute | solution.py:203
  347.5 5.9 %collective-permute-start.5 = (f32[1]{0:T(128)}, f32[1]{0:T(128)}, u32[]{:S(2)}, u32[]{:S(2)}) collective-permute-start(f32[1]{0:T(128)} %collective-permute-done.3), channel_id=1, source_target_pairs={{16,0},{32,16},{48,32},{64,48},{80,64},{96,80},{112,96},{128,112},... | collective-permute-start | bytes 20 | tf_op jit(solution)/shard_map/ppermute | solution.py:203
  354.2 6.0 %collective-permute-start.7 = (f32[1]{0:T(128)}, f32[1]{0:T(128)}, u32[]{:S(2)}, u32[]{:S(2)}) collective-permute-start(f32[1]{0:T(128)} %collective-permute-done.5), channel_id=1, source_target_pairs={{16,0},{32,16},{48,32},{64,48},{80,64},{96,80},{112,96},{128,112},... | collective-permute-start | bytes 20 | tf_op jit(solution)/shard_map/ppermute | solution.py:203
  361.1 5.9 %collective-permute-start.9 = (f32[1]{0:T(128)}, f32[1]{0:T(128)}, u32[]{:S(2)}, u32[]{:S(2)}) collective-permute-start(f32[1]{0:T(128)} %collective-permute-done.7), channel_id=1, source_target_pairs={{16,0},{32,16},{48,32},{64,48},{80,64},{96,80},{112,96},{128,112},... | collective-permute-start | bytes 20 | tf_op jit(solution)/shard_map/ppermute | solution.py:203
  369.2 129.6 %all-reduce.3.cloned.1.call-done = (f32[512,512]{1,0:T(8,128)}, f32[512,512]{1,0:T(8,128)}, f32[512,512]{1,0:T(8,128)}, f32[512,512]{1,0:T(8,128)}, f32[512,512]{1,0:T(8,128)}, /*index=5*/f32[512,512]{1,0:T(8,128)}) async-done(((f32[512,512]{1,0:T(8,128)}, f32[512,512]{1,0:T(8,128)}, f32[512,512]{1,0:T(8,128)}, f32[512,512]{1,0:T(8,128)}, f32[512,512]{1,0:T(8,128)}, /*index=5*/f32[512,512]{1,0:T(8,128)}), ...) | async-done | bytes 6291472 | tf_op jit(solution)/shard_map/psum | solution.py:225
  514.7 13.7 %multiply_reduce_fusion = (f32[]{:T(128)}, f32[]{:T(128)}, f32[]{:T(128)}, f32[]{:T(128)}) fusion(f32[512,512]{1,0:T(8,128)} %copy.16, f32[512,512]{1,0:T(8,128)} %get-tuple-element.14, f32[512]{0:T(512)S(1)} %copy-done.21, f32[512]{0:T(512)S(1)} %get-tuple-element.21, f32[512,512]{1,0:T(8,128)} %copy.13, f32[512,512]{1,0:T(8,128)} %get-tuple-element.11, ...), kind=kLoop, calls=%fused_computation.12 | loop fusion | flops 6291452 | bytes 8398864 | tf_op jit(solution)/shard_map/reduce_sum | solution.py:227
  536.1 4.4 fusion.13
  543.3 4.1 convolution_add_fusion.4
  (70 shorter events, 43.6 us)
Async XLA Ops:
  7.2 491.6 %all-reduce.3.cloned.1.call-start = ((), (), s32[]{:S(2)}) async-start(), calls=%async_computation | async-start | bytes 12582912 | tf_op jit(solution)/shard_map/psum | solution.py:225
  96.6 48.4 %collective-permute-start = (f32[512,512]{1,0:T(8,128)S(1)}, f32[512,512]{1,0:T(8,128)S(1)}, u32[]{:S(2)}, u32[]{:S(2)}) collective-permute-start(f32[512,512]{1,0:T(8,128)S(1)} %shard_map.59), channel_id=1, source_target_pairs={{16,0},{32,16},{48,32},{64,48},{80,64},{96,80},{112,96},{128,112},... | collective-permute-start | bytes 3145736 | tf_op jit(solution)/shard_map/ppermute | solution.py:203
  145.0 147.0 %copy-start.12 = (f32[512,512]{1,0:T(8,128)}, f32[512,512]{1,0:T(8,128)S(1)}, u32[]{:S(2)}) copy-start(f32[512,512]{1,0:T(8,128)S(1)} %collective-permute-done) | copy-start | bytes 3145732
  145.0 37.6 %collective-permute-start.2 = (f32[512,512]{1,0:T(8,128)S(1)}, f32[512,512]{1,0:T(8,128)S(1)}, u32[]{:S(2)}, u32[]{:S(2)}) collective-permute-start(f32[512,512]{1,0:T(8,128)S(1)} %collective-permute-done), channel_id=1, source_target_pairs={{16,0},{32,16},{48,32},{64,48},{80,64},{96,80},{112,96},{128,112},... | collective-permute-start | bytes 3145736 | tf_op jit(solution)/shard_map/ppermute | solution.py:203
  182.6 112.2 %copy-start.13 = (f32[512,512]{1,0:T(8,128)}, f32[512,512]{1,0:T(8,128)S(1)}, u32[]{:S(2)}) copy-start(f32[512,512]{1,0:T(8,128)S(1)} %collective-permute-done.2) | copy-start | bytes 3145732
  182.6 50.4 %collective-permute-start.4 = (f32[512,512]{1,0:T(8,128)S(1)}, f32[512,512]{1,0:T(8,128)S(1)}, u32[]{:S(2)}, u32[]{:S(2)}) collective-permute-start(f32[512,512]{1,0:T(8,128)S(1)} %collective-permute-done.2), channel_id=1, source_target_pairs={{16,0},{32,16},{48,32},{64,48},{80,64},{96,80},{112,96},{128,112},... | collective-permute-start | bytes 3145736 | tf_op jit(solution)/shard_map/ppermute | solution.py:203
  233.0 64.7 %copy-start.15 = (f32[512,512]{1,0:T(8,128)}, f32[512,512]{1,0:T(8,128)S(1)}, u32[]{:S(2)}) copy-start(f32[512,512]{1,0:T(8,128)S(1)} %collective-permute-done.4) | copy-start | bytes 3145732
  233.0 52.3 %collective-permute-start.6 = (f32[512,512]{1,0:T(8,128)S(1)}, f32[512,512]{1,0:T(8,128)S(1)}, u32[]{:S(2)}, u32[]{:S(2)}) collective-permute-start(f32[512,512]{1,0:T(8,128)S(1)} %collective-permute-done.4), channel_id=1, source_target_pairs={{16,0},{32,16},{48,32},{64,48},{80,64},{96,80},{112,96},{128,112},... | collective-permute-start | bytes 3145736 | tf_op jit(solution)/shard_map/ppermute | solution.py:203
  285.3 15.2 %copy-start.17 = (f32[512,512]{1,0:T(8,128)}, f32[512,512]{1,0:T(8,128)S(1)}, u32[]{:S(2)}) copy-start(f32[512,512]{1,0:T(8,128)S(1)} %collective-permute-done.6) | copy-start | bytes 3145732
  285.3 44.4 %collective-permute-start.8 = (f32[512,512]{1,0:T(8,128)S(1)}, f32[512,512]{1,0:T(8,128)S(1)}, u32[]{:S(2)}, u32[]{:S(2)}) collective-permute-start(f32[512,512]{1,0:T(8,128)S(1)} %collective-permute-done.6), channel_id=1, source_target_pairs={{16,0},{32,16},{48,32},{64,48},{80,64},{96,80},{112,96},{128,112},... | collective-permute-start | bytes 3145736 | tf_op jit(solution)/shard_map/ppermute | solution.py:203
  333.5 7.4 %collective-permute-start.1 = (f32[1]{0:T(128)}, f32[1]{0:T(128)}, u32[]{:S(2)}, u32[]{:S(2)}) collective-permute-start(f32[1]{0:T(128)} %param.6), channel_id=1, source_target_pairs={{16,0},{32,16},{48,32},{64,48},{80,64},{96,80},{112,96},{128,112},... | collective-permute-start | bytes 20 | tf_op jit(solution)/shard_map/ppermute | solution.py:203
  340.9 6.6 %collective-permute-start.3 = (f32[1]{0:T(128)}, f32[1]{0:T(128)}, u32[]{:S(2)}, u32[]{:S(2)}) collective-permute-start(f32[1]{0:T(128)} %collective-permute-done.1), channel_id=1, source_target_pairs={{16,0},{32,16},{48,32},{64,48},{80,64},{96,80},{112,96},{128,112},... | collective-permute-start | bytes 20 | tf_op jit(solution)/shard_map/ppermute | solution.py:203
  347.5 6.6 %collective-permute-start.5 = (f32[1]{0:T(128)}, f32[1]{0:T(128)}, u32[]{:S(2)}, u32[]{:S(2)}) collective-permute-start(f32[1]{0:T(128)} %collective-permute-done.3), channel_id=1, source_target_pairs={{16,0},{32,16},{48,32},{64,48},{80,64},{96,80},{112,96},{128,112},... | collective-permute-start | bytes 20 | tf_op jit(solution)/shard_map/ppermute | solution.py:203
  354.2 7.0 %collective-permute-start.7 = (f32[1]{0:T(128)}, f32[1]{0:T(128)}, u32[]{:S(2)}, u32[]{:S(2)}) collective-permute-start(f32[1]{0:T(128)} %collective-permute-done.5), channel_id=1, source_target_pairs={{16,0},{32,16},{48,32},{64,48},{80,64},{96,80},{112,96},{128,112},... | collective-permute-start | bytes 20 | tf_op jit(solution)/shard_map/ppermute | solution.py:203
  361.1 6.7 %collective-permute-start.9 = (f32[1]{0:T(128)}, f32[1]{0:T(128)}, u32[]{:S(2)}, u32[]{:S(2)}) collective-permute-start(f32[1]{0:T(128)} %collective-permute-done.7), channel_id=1, source_target_pairs={{16,0},{32,16},{48,32},{64,48},{80,64},{96,80},{112,96},{128,112},... | collective-permute-start | bytes 20 | tf_op jit(solution)/shard_map/ppermute | solution.py:203
  498.8 2.7 copy-start.2
  498.8 2.7 copy-start.3
  536.1 4.4 copy-start.7
  536.1 4.4 copy-start.9
  536.1 4.4 copy-start.10
  536.1 4.4 copy-start.11
  543.3 4.2 copy-start.6
  543.3 4.2 copy-start.14
  549.6 2.1 copy-start.4
  (9 other events, 14.1 us)
Sparse Core Ops, SparseCore 0:
  333.6 165.0 all-reduce.2

commit v2 on v1

--- a/solution.py
+++ b/solution.py
@@ -35,7 +35,7 @@
     pl.semaphore_wait(barrier, len(peers))
 
 
-def fit_kernel(fit_ref, int_ref, out_ref, fb, ib, fsend, frecv, isend, irecv):
+def fit_kernel(fit_ref, int_ref, out_ref, acc, fb, ib, fsend, frecv, isend, irecv):
     at = Place()
     me = (at.occ, at.fit)
     entry_barrier(
@@ -129,7 +129,7 @@
 
         def one(k, carry):
             slot = at.o(k, dy)
-            out_ref[...] += jnp.dot(fb[slot], ib[slot], preferred_element_type=jnp.float32)
+            acc[...] += jnp.dot(fb[slot], ib[slot], preferred_element_type=jnp.float32)
             return carry
 
         lax.fori_loop(0, 4, one, 0)
@@ -141,7 +141,7 @@
     to_core(int_ref, at.fit)
     fb[at.occ] = fit_ref[...]
     ib[at.fit] = int_ref[...]
-    out_ref[...] = jnp.zeros_like(out_ref)
+    acc[...] = jnp.zeros_like(acc)
 
     f_relay_y(0)
     i_relay(0)
@@ -172,6 +172,9 @@
     multiply(1)
     multiply(3)
     multiply(2)
+    hi = acc[...].astype(jnp.bfloat16)
+    out_ref[0] = hi
+    out_ref[1] = (acc[...] - hi.astype(jnp.float32)).astype(jnp.bfloat16)
     for copy in started:
         copy.wait_send()
 
@@ -180,10 +183,11 @@
     sends = 37
     return pl.pallas_call(
         fit_kernel,
-        out_shape=jax.ShapeDtypeStruct((512, 512), jnp.float32),
+        out_shape=jax.ShapeDtypeStruct((2, 512, 512), jnp.bfloat16),
         in_specs=[pl.BlockSpec(memory_space=pltpu.VMEM)] * 2,
         out_specs=pl.BlockSpec(memory_space=pltpu.VMEM),
         scratch_shapes=[
+            pltpu.VMEM((512, 512), jnp.float32),
             pltpu.VMEM((16, 512, 512), jnp.bfloat16),
             pltpu.VMEM((16, 512, 512), jnp.bfloat16),
             pltpu.SemaphoreType.DMA((sends,)),
@@ -197,41 +201,306 @@
     )(fitting, integrals)
 
 
-def passed_along(block, axis, distance):
-    devices = range(lax.axis_size(axis))
-    route = [((i - distance) % len(devices), i) for i in devices]
-    return lax.ppermute(block, axis, route)
+ORDER = (0, 4, 1, 3, 2, 5)
+SLOT = {d: k for k, d in enumerate(ORDER)}
+SPARE = 6
+CHUNKS = 4
+ROUTES = (
+    (0, SLOT[4], -1, 0),
+    (0, SLOT[1], 0, -1),
+    (0, SLOT[3], 0, 1),
+    (SLOT[1], SLOT[2], 0, -1),
+    (SLOT[1], SLOT[5], -1, 0),
+    (SLOT[4], SLOT[3], 0, 1),
+    (SLOT[4], SLOT[5], 0, -1),
+    (SLOT[4], SLOT[1], 0, -1),
+    (SLOT[4], SPARE, -1, 0),
+    (SLOT[3], SLOT[2], 0, 1),
+    (SLOT[2], SLOT[5], 0, 1),
+    (SPARE, SLOT[5], 0, -1),
+)
+
+
+def takes(route, y, c):
+    return (
+        True,
+        y > 0,
+        y == 3,
+        y == 1,
+        (y == 3) & (c < 2),
+        y < 3,
+        y >= 2,
+        y == 0,
+        (y == 0) & (c >= 2),
+        y < 3,
+        y == 3,
+        (y == 0) & (c >= 2),
+    )[route]
+
+
+def dot_nt(a, b):
+    return lax.dot_general(a, b, (((1,), (1,)), ((), ())), preferred_element_type=jnp.float32)
+
+
+def dot_nn(a, b):
+    return jnp.dot(a, b, preferred_element_type=jnp.float32)
+
+
+def pair_kernel(
+    own_ref, occ_ref, vrow_ref, vcol_ref, out_ref, en_ref,
+    pt, spare, ownt, pbo, hb, cb, xb, qb, zb, am, eb,
+    rs, rr, es, er, cs, cr, xs, xr, zs, zr, azs, azr, axs, axr, acs, acr,
+):
+    at = Place()
+    y = at.y
+    core_peer, low_peer = at.f(0, 0, 1), at.f(0, 1)
+    x_peers = (at.f(1), at.f(-1), at.f(2))
+    ahead = [(at.occ + d) % 16 for d in range(1, 6)]
+    behind = [(at.occ + 16 - d) % 16 for d in range(1, 6)]
+    entry_barrier(
+        [(o, at.fit) for o in ahead + behind]
+        + [(at.occ, f) for f in x_peers + (core_peer, low_peer)]
+    )
+
+    def remote(src, dst, ssem, rsem, occ, fit):
+        return pltpu.make_async_remote_copy(
+            src_ref=src, dst_ref=dst, send_sem=ssem, recv_sem=rsem,
+            device_id={"occ": occ, "fit": fit}, device_id_type=MESH,
+        )
+
+    def rows(c):
+        return pl.ds(pl.multiple_of(c * 128, 128), 128)
+
+    def place(slot, c):
+        if slot == SPARE:
+            return spare.at[:, pl.ds(pl.multiple_of((c - 2) * 128, 128), 128)]
+        return pt.at[slot, :, rows(c)]
+
+    def route(n, c):
+        src, dst, dz, dy = ROUTES[n]
+        return remote(
+            own_ref.at[:, rows(c)] if src == 0 else place(src, c),
+            place(dst, c), rs.at[n, c], rr.at[dst, c], at.o(dz, dy), at.fit,
+        )
+
+    def send_on(slot, c):
+        for n in range(len(ROUTES)):
+            if ROUTES[n][0] == slot:
+                pl.when(takes(n, y, c))(lambda n=n: route(n, c).start())
+
+    def got(slot, c):
+        part = place(slot, c)
+        remote(part, part, rs.at[0, 0], rr.at[slot, c], at.occ, at.fit).wait_recv()
+
+    def energy_copy(d):
+        k = SLOT[d]
+        return remote(occ_ref, eb.at[k], es.at[k], er.at[k], behind[d - 1], at.fit)
+
+    mine = pl.ds(pl.multiple_of(at.core * 256, 256), 256)
+    other = pl.ds(pl.multiple_of((1 - at.core) * 256, 256), 256)
+
+    def quarter(x):
+        return pl.ds(pl.multiple_of(x * 64, 64), 64)
+
+    def core_copy(k):
+        return remote(pbo.at[k], cb.at[k], cs.at[k], cr.at[k], at.occ, core_peer)
+
+    def x_copy(k, n):
+        to = (at.x + (1, 3, 2)[n]) % 4
+        return remote(hb.at[k, quarter(to)], xb.at[k, n], xs.at[k, n], xr.at[k, n], at.occ, x_peers[n])
+
+    def z_copy(k):
+        half = pl.ds(pl.multiple_of((1 - at.low) * 32, 32), 32)
+        return remote(qb.at[k, half], zb.at[k], zs.at[k], zr.at[k], at.occ, low_peer)
+
+    def block(x, core):
+        return pl.ds(pl.multiple_of(core * 256 + x * 64, 64), 64)
+
+    own_rows = pl.ds(pl.multiple_of(at.core * 256 + at.x * 64 + at.low * 32, 32), 32)
+
+    def az_copy(k):
+        part = am.at[k, :, own_rows]
+        return remote(part, part, azs.at[k], azr.at[k], at.occ, low_peer)
+
+    def ax_copy(k, n):
+        part = am.at[k, :, block(at.x, at.core)]
+        return remote(part, part, axs.at[k, n], axr.at[k, n], at.occ, x_peers[n])
+
+    def ac_copy(k, n):
+        part = am.at[k, :, block((at.x + n) % 4, at.core)]
+        return remote(part, part, acs.at[k, n], acr.at[k, n], at.occ, core_peer)
+
+    def c1(k):
+        @pl.when(k == 5)
+        def _():
+            for c in range(CHUNKS):
+                got(SLOT[5], c)
+
+        hi, lo = pt[k, 0], pt[k, 1]
+
+        def part(where):
+            return (
+                dot_nn(ownt[0, where], hi) + dot_nn(ownt[0, where], lo) + dot_nn(ownt[1, where], hi)
+            )
+
+        pbo[k] = part(other)
+        core_copy(k).start()
+        hb[k] = part(mine)
+
+    def c2(k):
+        core_copy(k).wait_recv()
+        hb[k] += cb[k]
+        for n in range(3):
+            x_copy(k, n).start()
+
+    def c3(k):
+        for n in range(3):
+            x_copy(k, n).wait_recv()
+        qb[k] = (hb[k, quarter(at.x)] + xb[k, 0]) + (xb[k, 1] + xb[k, 2])
+        z_copy(k).start()
+
+    def c4(k):
+        z_copy(k).wait_recv()
+        summed = qb[k, pl.ds(pl.multiple_of(at.low * 32, 32), 32)] + zb[k]
+        energy = occ_ref[0:1, 0:1] + eb[k, 0:1, 0:1]
+        denom = energy - vcol_ref[own_rows] - vrow_ref[...]
+        amplitude = summed / denom
+        hi = amplitude.astype(jnp.bfloat16)
+        am[k, 0, own_rows] = hi
+        am[k, 1, own_rows] = (amplitude - hi.astype(jnp.float32)).astype(jnp.bfloat16)
+        az_copy(k).start()
+
+    def c5(k):
+        az_copy(k).wait_recv()
+        for n in range(3):
+            ax_copy(k, n).start()
+        ac_copy(k, 0).start()
+
+    def c6(k):
+        for n in range(3):
+            ax_copy(k, n).wait_recv()
+            ac_copy(k, (3, 1, 2)[n]).start()
+
+    def c7(k):
+        for n in range(4):
+            ac_copy(k, n).wait_recv()
+        hi, lo = pt[k, 0], pt[k, 1]
+        out_ref[...] += dot_nt(hi, am[k, 0]) + dot_nt(hi, am[k, 1]) + dot_nt(lo, am[k, 0])
+        energy = occ_ref[0:1, 0:1] + eb[k, 0:1, 0:1]
+        total = jnp.zeros((1, 1), jnp.float32)
+        for r in range(4):
+            band = pl.ds(r * 128, 128)
+            a = am[k, 0, band].astype(jnp.float32) + am[k, 1, band].astype(jnp.float32)
+            b = am[k, 0, :, band].astype(jnp.float32) + am[k, 1, :, band].astype(jnp.float32)
+            denom = energy - vcol_ref[band] - vrow_ref[...]
+            total += jnp.sum(a * denom * (2.0 * a - b.T), axis=(0, 1), keepdims=True)
+        line = lax.broadcasted_iota(jnp.int32, en_ref.shape, 0)
+        en_ref[...] += jnp.where(line == k, total, 0.0)
+
+    for d in range(1, 6):
+        energy_copy(d).start()
+    for c in range(CHUNKS):
+        send_on(0, c)
+    pt[0] = own_ref[...]
+    eb[0] = occ_ref[...]
+    ownt[0] = own_ref[0].astype(jnp.float32).T.astype(jnp.bfloat16)
+    ownt[1] = own_ref[1].astype(jnp.float32).T.astype(jnp.bfloat16)
+    out_ref[...] = jnp.zeros_like(out_ref)
+    en_ref[...] = jnp.zeros_like(en_ref)
+    for d in range(1, 6):
+        energy_copy(d).wait_recv()
+
+    def step(r, carry):
+        for slot, first in ((SLOT[4], 0), (SLOT[1], 0), (SLOT[3], 1), (SLOT[2], 2)):
+            c = r - first
+
+            @pl.when((c >= 0) & (c < CHUNKS))
+            def _():
+                got(slot, c)
+                send_on(slot, c)
+
+        c = r - 3
+
+        @pl.when((c >= 2) & (c < CHUNKS) & (y == 0))
+        def _():
+            got(SPARE, c)
+            send_on(SPARE, c)
+
+        for j, stage in ((1, c2), (2, c3), (3, c4), (4, c5), (5, c6), (0, c1), (6, c7)):
+            turn = r - j
+
+            @pl.when((turn == 0) | ((turn >= 4) & (turn <= 8)))
+            def _():
+                stage(jnp.where(turn == 0, 0, turn - 3))
+
+        return carry
+
+    lax.fori_loop(0, 15, step, 0)
+
+    for n in range(len(ROUTES)):
+        for c in range(CHUNKS):
+            pl.when(takes(n, y, c))(lambda n=n, c=c: route(n, c).wait_send())
+    for d in range(1, 6):
+        energy_copy(d).wait_send()
+
+    def finish(k, carry):
+        core_copy(k).wait_send()
+        z_copy(k).wait_send()
+        az_copy(k).wait_send()
+        for n in range(3):
+            x_copy(k, n).wait_send()
+            ax_copy(k, n).wait_send()
+        for n in range(4):
+            ac_copy(k, n).wait_send()
+        return carry
+
+    lax.fori_loop(0, 6, finish, 0)
+
+
+def pairs_of(fitted, occ_tile, vir_row, vir_col):
+    f32, bf16 = jnp.float32, jnp.bfloat16
+    dma = pltpu.SemaphoreType.DMA
+    return pl.pallas_call(
+        pair_kernel,
+        out_shape=(
+            jax.ShapeDtypeStruct((512, 512), f32),
+            jax.ShapeDtypeStruct((8, 128), f32),
+        ),
+        in_specs=[pl.BlockSpec(memory_space=pltpu.VMEM)] * 4,
+        out_specs=[pl.BlockSpec(memory_space=pltpu.VMEM)] * 2,
+        scratch_shapes=[
+            pltpu.VMEM((6, 2, 512, 512), bf16),
+            pltpu.VMEM((2, 256, 512), bf16),
+            pltpu.VMEM((2, 512, 512), bf16),
+            pltpu.VMEM((6, 256, 512), f32),
+            pltpu.VMEM((6, 256, 512), f32),
+            pltpu.VMEM((6, 256, 512), f32),
+            pltpu.VMEM((6, 3, 64, 512), f32),
+            pltpu.VMEM((6, 64, 512), f32),
+            pltpu.VMEM((6, 32, 512), f32),
+            pltpu.VMEM((6, 2, 512, 512), bf16),
+            pltpu.VMEM((6, 8, 128), f32),
+            dma((len(ROUTES), CHUNKS)), dma((7, CHUNKS)),
+            dma((6,)), dma((6,)),
+            dma((6,)), dma((6,)),
+            dma((6, 3)), dma((6, 3)),
+            dma((6,)), dma((6,)),
+            dma((6,)), dma((6,)),
+            dma((6, 3)), dma((6, 3)),
+            dma((6, 4)), dma((6, 4)),
+        ],
+        compiler_params=pltpu.CompilerParams(
+            collective_id=1, has_side_effects=True, vmem_limit_bytes=56 * 1024 * 1024
+        ),
+    )(fitted, occ_tile, vir_row, vir_col)
 
 
 def body(integrals, fitting, occ_energy, vir_energy):
     nvir = integrals.shape[2]
     fitted = fitted_of(fitting, integrals[:, 0, :])
-    own_energy = occ_energy[0]
-    partner = fitted
-    partner_energy = occ_energy
-    density = jnp.zeros_like(fitted)
-    energies = []
-    for step in range(STOPS):
-        if step > 0:
-            partner, partner_energy = passed_along((partner, partner_energy), "occ", -1)
-        local_pair = lax.dot_general(
-            fitted,
-            partner,
-            (((0,), (0,)), ((), ())),
-            precision=lax.Precision.HIGHEST,
-            preferred_element_type=jnp.float32,
-        )
-        denom = own_energy + partner_energy[0] - vir_energy[:, None] - vir_energy[None, :]
-        summed = lax.psum(local_pair, "fit")
-        amplitude = summed / denom
-        energies.append(jnp.sum(amplitude * (2.0 * summed - summed.T)) / (nvir * nvir))
-        density = density + jnp.dot(
-            partner,
-            amplitude.T,
-            precision=lax.Precision.HIGHEST,
-            preferred_element_type=jnp.float32,
-        )
-    pair_energy = jnp.stack(energies)[None, :]
+    occ_tile = jnp.broadcast_to(occ_energy[:, None], (8, 128))
+    density, energies = pairs_of(fitted, occ_tile, vir_energy[None, :], vir_energy[:, None])
+    pair_energy = jnp.stack([energies[SLOT[d], 0] for d in range(STOPS)])[None, :] / (nvir * nvir)
     return (density[:, None, :], pair_energy)
 
 

time: 573 us -> 255 us (0.45)
  waiting for transfers between devices: 320 us -> 0 us
  Pallas kernels: 87.3 us -> 236 us
  starting transfers between devices: 59.4 us -> 0 us
  matrix products: 33.8 us -> 0 us
  between operations: 22.3 us -> 1.32 us
  other arithmetic: 16.8 us -> 0.52 us
  local copies, waits for them, and re-layouts: 25.9 us -> 12.4 us
    ppermute x10 -> x0, waiting for transfers between devices: 190 us -> none  [passed_along(): return lax.ppermute(block, axis, route)]
    pallas_call x1 -> x2, Pallas kernels: 87.3 us -> 236 us  [the longest x1 148 us: pairs_of(): pl.pallas_call(pair_kernel, out_shape=(jax.ShapeDtypeStruct((512, 512), f...]
    psum x1 -> x0, waiting for transfers between devices: 130 us -> none  [body(): summed = lax.psum(local_pair, 'fit')]
    ppermute x10 -> x0, starting transfers between devices: 59.3 us -> none  [passed_along(): return lax.ppermute(block, axis, route)]
    dot_general x12 -> x0, matrix products: 33.8 us -> none  [the longest x6 17.1 us: body(): lax.dot_general(fitted, partner, (((0,), (0,)), ((), ())), precision=lax....]
    reduce_sum x2 -> x0, other arithmetic: 15.2 us -> none  [body(): jnp.sum(amplitude * (2.0 * summed - summed.T)) / (nvir * nvir)]
    transpose x4 -> x0, local copies, waits for them, and re-layouts: 10.2 us -> none  [body(): energies.append(jnp.sum(amplitude * (2.0 * summed - summed.T)) / (nvir *...]
  transfers between devices with their start and end apart: 11 -> 0, of which waited for: 11 -> 0; matrix products, arithmetic and copies ran while one was open for 3% -> 0% of each run, Pallas kernels for 0% -> 0%
where the time goes in v2:
time: 255 us; the launch traced here: 250 us
  Pallas kernels  236 us (93%)
  local copies, waits for them, and re-layouts  12.4 us (5%)
    pallas_call x1, Pallas kernels, pairs_of(): pl.pallas_call(pair_kernel, out_shape=(jax.ShapeDtypeStruct((512, 512), f...  148 us
    pallas_call x1, Pallas kernels, fitted_of(): pl.pallas_call(fit_kernel, out_shape=jax.ShapeDtypeStruct((2, 512, 512),...  87.4 us
    unnamed x11, local copies, waits for them, and re-layouts  6.41 us

profile of v2, /device:TPU:1, one launch (start us, length us, event | category | flops | bytes accessed | tf_op | source)
XLA Modules:
  0.0 250.1 jit_solution(5253578672502903517)
XLA Ops:
  1.3 0.0 copy-start.3
  1.3 0.6 broadcast_in_dim.19.occ_ref
  1.9 0.1 copy-done.3
  2.0 0.9 copy.7.vcol_ref
  2.8 0.0 copy-start.1
  2.8 1.0 copy-done.1
  3.9 0.0 copy-start.2
  3.9 1.0 copy-done.2
  4.9 87.4 %shard_map.59.own_ref = bf16[2,512,512]{2,1,0:T(8,128)(2,1)S(1)} custom-call(bf16[512,512]{1,0:T(8,128)(2,1)S(1)} %copy-done.1, bf16[512,512]{1,0:T(8,128)(2,1)S(1)} %bitcast.6), custom_call_target="tpu_custom_call" | custom-call | tf_op jit(solution)/shard_map/pallas_call | solution.py:184
  92.4 0.0 copy-start
  92.4 1.0 copy-done
  93.3 148.4 %shard_map.60 = (f32[512,512]{1,0:T(8,128)}, f32[8,128]{1,0:T(8,128)}) custom-call(bf16[2,512,512]{2,1,0:T(8,128)(2,1)} %copy-done, f32[8,128]{1,0:T(8,128)} %broadcast_in_dim.19.occ_ref, f32[1,512]{1,0:T(1,128)} %bitcast.8, f32[512,1]{1,0:T(8,128)} %copy.7.vcol_ref), custom_call_target="tpu_custom_call" | custom-call | tf_op jit(solution)/shard_map/pallas_call | solution.py:463
  241.7 0.0 copy-start.4
  241.7 3.3 %copy.8 = f32[512,1,512]{2,1,0:T(1,128)} copy(f32[512,1,512]{2,0,1:T(8,128)} %bitcast.7) | data formatting | bytes 2097152
  245.0 0.0 copy-done.4
  245.0 0.6 fusion
  245.6 3.9 %stack.3 = f32[1,6]{1,0:T(1,128)S(1)} concatenate(f32[1,1]{1,0:T(1,128)} %get-tuple-element.15, f32[1,1]{1,0:T(1,128)} %get-tuple-element.14, f32[1,1]{1,0:T(1,128)} %get-tuple-element.13, f32[1,1]{1,0:T(1,128)} %get-tuple-element.12, f32[1,1]{1,0:T(1,128)} %get-tuple-element.11, f32[1,1]{1,0:T(1,128)} %get-tuple-element.10), dimensions={1} | concatenate | bytes 48 | tf_op jit(solution)/shard_map/stack | solution.py:503
  249.5 0.5 broadcast_multiply_fusion
Async XLA Ops:
  1.3 0.7 copy-start.3
  2.8 1.0 copy-start.1
  3.9 1.0 copy-start.2
  92.4 1.0 copy-start
  241.7 3.3 %copy-start.4 = (f32[8,128]{1,0:T(8,128)S(1)}, f32[8,128]{1,0:T(8,128)}, u32[]{:S(2)}) copy-start(f32[8,128]{1,0:T(8,128)} %get-tuple-element.5) | copy-start | bytes 12292

commit v3 on v2

v3 whole, which is shorter than its diff:
```python
import jax
import jax.numpy as jnp
from jax import lax
from jax.experimental import pallas as pl
from jax.experimental.pallas import tpu as pltpu
from jax.sharding import PartitionSpec as P

STOPS = 6
MESH = pl.DeviceIdType.MESH


class Place:
    def __init__(self):
        self.occ = lax.axis_index("occ")
        self.fit = lax.axis_index("fit")
        self.z, self.y = self.occ // 4, self.occ % 4
        self.x, self.low, self.core = self.fit // 4, (self.fit // 2) % 2, self.fit % 2

    def o(self, dz, dy):
        return ((self.z + dz + 4) % 4) * 4 + (self.y + dy + 4) % 4

    def f(self, dx, flip_low=0, flip_core=0):
        low = self.low if not flip_low else 1 - self.low
        core = self.core if not flip_core else 1 - self.core
        return ((self.x + dx + 4) % 4) * 4 + low * 2 + core


def entry_barrier(peers):
    barrier = pltpu.get_barrier_semaphore()
    for occ, fit in peers:
        pl.semaphore_signal(barrier, inc=1, device_id={"occ": occ, "fit": fit}, device_id_type=MESH)
    pl.semaphore_wait(barrier, len(peers))


ORDER = (0, 4, 1, 3, 2, 5)
SLOT = {d: k for k, d in enumerate(ORDER)}
VIA, NEXT = 6, 7
CHUNKS = 4
ROUTES = (
    (0, SLOT[4], -1, 0),
    (0, SLOT[1], 0, -1),
    (0, SLOT[3], 0, 1),
    (0, VIA, 0, -1),
    (0, VIA, 1, 0),
    (SLOT[1], SLOT[2], 0, -1),
    (SLOT[4], SLOT[1], 0, -1),
    (SLOT[4], SLOT[3], 0, 1),
    (SLOT[4], SLOT[5], 0, -1),
    (SLOT[3], SLOT[2], 0, 1),
    (SLOT[2], SLOT[5], 0, 1),
    (VIA, NEXT, 1, 0),
    (NEXT, SLOT[5], 1, 0),
    (NEXT, SLOT[5], 0, -1),
)
HOPS = (
    (0, 0, None, "low"),
    (0, 0, None, 1),
    (0, 0, None, -1),
    (0, 0, None, "core"),
    (0, 1, None, 1),
    (0, 1, None, -1),
    (0, 1, None, "core"),
    (1, 0, 0, -1),
    (1, 0, None, "core"),
    (-1, 0, 1, 1),
    (-1, 0, None, "core"),
    (1, 1, 0, -1),
    (1, 1, None, "core"),
    (-1, 1, 1, 1),
    (-1, 1, None, "core"),
    (2, 0, None, "core"),
    (2, 1, None, "core"),
)


def carries(y, c):
    return ((y == 3) & (c < 2)) | ((y == 0) & (c >= 2))


def takes(route, y, c):
    return (
        True,
        y > 0,
        y == 3,
        (y == 0) & (c < 2),
        (y == 0) & (c >= 2),
        y == 1,
        y == 0,
        y < 3,
        y >= 2,
        y < 3,
        y == 3,
        carries(y, c),
        (y == 3) & (c < 2),
        (y == 0) & (c >= 2),
    )[route]


def dot_nt(a, b):
    return lax.dot_general(a, b, (((1,), (1,)), ((), ())), preferred_element_type=jnp.float32)


def dot_nn(a, b):
    return jnp.dot(a, b, preferred_element_type=jnp.float32)


def kernel(
    fit_ref, int_ref, occ_ref, vir_ref, out_ref, en_ref,
    fb, ib, acc, pt, spare, ownt, pbo, hb, cb, xb, qb, zb, am, eb, vcol,
    fs, fr, js, jr, rs, rr, es, er, cs, cr, xs, xr, zs, zr, azs, azr, axs, axr, acs, acr,
):
    at = Place()
    y = at.y
    core_peer, low_peer = at.f(0, 0, 1), at.f(0, 1)
    x_peers = (at.f(1), at.f(-1), at.f(2))
    ahead = [(at.occ + d) % 16 for d in range(1, 6)]
    behind = [(at.occ + 16 - d) % 16 for d in range(1, 6)]
    entry_barrier(
        [(o, at.fit) for o in ahead + behind]
        + [(at.occ, f) for f in x_peers + (core_peer, low_peer)]
    )

    def remote(src, dst, ssem, rsem, occ, fit):
        return pltpu.make_async_remote_copy(
            src_ref=src, dst_ref=dst, send_sem=ssem, recv_sem=rsem,
            device_id={"occ": occ, "fit": fit}, device_id_type=MESH,
        )

    def rows(c):
        return pl.ds(pl.multiple_of(c * 128, 128), 128)

    def rows_of(c, half):
        if half is None:
            return rows(c)
        return pl.ds(pl.multiple_of(c * 128 + half * 64, 64), 64)

    def f_copy(n, c):
        if n < 2:
            slot, half, own, to = at.occ, None, True, at.o((1, -1)[n], 0)
        elif n < 4:
            slot, half, own, to = at.o((1, -1)[n - 2], 0), n - 2, False, at.o((-1, 1)[n - 2], 0)
        elif n < 12:
            dz, up = (n - 4) // 2, (n - 4) % 2
            slot, half, own, to = at.o(dz, 0), None, dz == 0, at.o(0, (1, -1)[up])
        else:
            dz, up = (n - 12) // 2, (n - 12) % 2
            slot, half, own, to = at.o(dz, (1, -1)[up]), up, False, at.o(0, (-1, 1)[up])
        where = rows_of(c, half)
        src = fit_ref.at[where] if own else fb.at[slot, where]
        return remote(src, fb.at[slot, where], fs.at[n, c], fr.at[slot, c, half or 0], to, at.fit)

    def f_got(dz, dy, c):
        slot = at.o(dz, dy)
        for half in ((0, 1) if dy == 2 or (dz == 2 and dy == 0) else (None,)):
            part = fb.at[slot, rows_of(c, half)]
            remote(part, part, fs.at[0, 0], fr.at[slot, c, half or 0], at.occ, at.fit).wait_recv()

    def f_spread(dz, c):
        f_copy(4 + 2 * dz, c).start()
        f_copy(5 + 2 * dz, c).start()

    def f_first(c):
        f_got(1, 0, c)
        f_copy(2, c).start()
        f_spread(1, c)
        f_got(3, 0, c)
        f_copy(3, c).start()
        f_spread(3, c)
        f_got(2, 0, c)
        f_spread(2, c)

    def f_second(c):
        for dz in (0, 1, 3, 2):
            f_got(dz, 1, c)
            f_copy(12 + 2 * dz, c).start()
            f_got(dz, 3, c)
            f_copy(13 + 2 * dz, c).start()

    def j_copy(n):
        dx, flip_low, half, to = HOPS[n]
        slot = at.f(dx, flip_low)
        where = pl.ds(0, 512) if half is None else pl.ds(half * 256, 256)
        src = int_ref.at[where] if (dx, flip_low) == (0, 0) else ib.at[slot, where]
        fit = {"low": low_peer, "core": core_peer, 1: at.f(1), -1: at.f(-1)}[to]
        return remote(src, ib.at[slot, where], js.at[n], jr.at[slot, half or 0], at.occ, fit)

    def j_send(*hops):
        for hop in hops:
            j_copy(HOPS.index(hop)).start()

    def j_got(slot, halves):
        for half in (0, 1) if halves else (None,):
            where = pl.ds(0, 512) if half is None else pl.ds(half * 256, 256)
            part = ib.at[slot, where]
            remote(part, part, js.at[0], jr.at[slot, half or 0], at.occ, at.fit).wait_recv()

    def j_relay(flip_low):
        for dx, half in ((1, 0), (-1, 1)):
            j_got(at.f(dx, flip_low), False)
            j_send((dx, flip_low, half, -dx), (dx, flip_low, None, "core"))

    def j_last(flip_low):
        j_got(at.f(2, flip_low), True)
        j_send((2, flip_low, None, "core"))

    def j_low():
        j_got(at.f(0, 1), False)
        j_send((0, 1, None, 1), (0, 1, None, -1), (0, 1, None, "core"))

    def j_core():
        for flip_low in (0, 1):
            for dx in (0, 1, -1, 2):
                j_got(at.f(dx, flip_low, 1), False)

    def place(slot, c):
        if slot >= VIA:
            return spare.at[slot - VIA, :, pl.ds(pl.multiple_of((c % 2) * 128, 128), 128)]
        return pt.at[slot, :, rows(c)]

    def route(n, c):
        src, dst, dz, dy = ROUTES[n]
        return remote(place(src, c), place(dst, c), rs.at[n, c], rr.at[dst, c], at.o(dz, dy), at.fit)

    def send_on(slot, c):
        for n in range(len(ROUTES)):
            if ROUTES[n][0] == slot:
                pl.when(takes(n, y, c))(lambda n=n: route(n, c).start())

    def got(slot, c):
        part = place(slot, c)
        remote(part, part, rs.at[0, 0], rr.at[slot, c], at.occ, at.fit).wait_recv()

    def energy_copy(d):
        k = SLOT[d]
        return remote(eb.at[0], eb.at[k], es.at[k], er.at[k], behind[d - 1], at.fit)

    def fit_chunk(c):
        def add(dy):
            def one(dz, carry):
                slot = at.o(dz, dy)
                acc[...] += dot_nn(fb[slot, rows(c)], ib[slot])
                return carry

            lax.fori_loop(0, 4, one, 0)

        acc[...] = jnp.zeros_like(acc)
        for dy in (0, 1, 3):
            add(dy)
        for dz in range(4):
            f_got(dz, 2, c)
        add(2)
        whole = acc[...]
        hi = whole.astype(jnp.bfloat16)
        low = whole - hi.astype(jnp.float32)
        pt[0, 0, rows(c)] = hi
        pt[0, 1, rows(c)] = low.astype(jnp.bfloat16)
        ownt[0, :, rows(c)] = hi.astype(jnp.float32).T.astype(jnp.bfloat16)
        ownt[1, :, rows(c)] = low.T.astype(jnp.bfloat16)
        send_on(0, c)

    mine = pl.ds(pl.multiple_of(at.core * 256, 256), 256)
    other = pl.ds(pl.multiple_of((1 - at.core) * 256, 256), 256)

    def quarter(x):
        return pl.ds(pl.multiple_of(x * 64, 64), 64)

    def core_copy(k):
        return remote(pbo.at[k], cb.at[k], cs.at[k], cr.at[k], at.occ, core_peer)

    def x_copy(k, n):
        to = (at.x + (1, 3, 2)[n]) % 4
        return remote(hb.at[k, quarter(to)], xb.at[k, n], xs.at[k, n], xr.at[k, n], at.occ, x_peers[n])

    def z_copy(k):
        half = pl.ds(pl.multiple_of((1 - at.low) * 32, 32), 32)
        return remote(qb.at[k, half], zb.at[k], zs.at[k], zr.at[k], at.occ, low_peer)

    def block(x, core):
        return pl.ds(pl.multiple_of(core * 256 + x * 64, 64), 64)

    own_rows = pl.ds(pl.multiple_of(at.core * 256 + at.x * 64 + at.low * 32, 32), 32)

    def az_copy(k):
        part = am.at[k, :, own_rows]
        return remote(part, part, azs.at[k], azr.at[k], at.occ, low_peer)

    def ax_copy(k, n):
        part = am.at[k, :, block(at.x, at.core)]
        return remote(part, part, axs.at[k, n], axr.at[k, n], at.occ, x_peers[n])

    def ac_copy(k, n):
        part = am.at[k, :, block((at.x + n) % 4, at.core)]
        return remote(part, part, acs.at[k, n], acr.at[k, n], at.occ, core_peer)

    def c1(k):
        @pl.when(k == 5)
        def _():
            for c in range(CHUNKS):
                got(SLOT[5], c)

        hi, lo = pt[k, 0], pt[k, 1]

        def part(where):
            return (
                dot_nn(ownt[0, where], hi) + dot_nn(ownt[0, where], lo) + dot_nn(ownt[1, where], hi)
            )

        pbo[k] = part(other)
        core_copy(k).start()
        hb[k] = part(mine)

    def c2(k):
        core_copy(k).wait_recv()
        hb[k] += cb[k]
        for n in range(3):
            x_copy(k, n).start()

    def c3(k):
        for n in range(3):
            x_copy(k, n).wait_recv()
        qb[k] = (hb[k, quarter(at.x)] + xb[k, 0]) + (xb[k, 1] + xb[k, 2])
        z_copy(k).start()

    def c4(k):
        z_copy(k).wait_recv()
        summed = qb[k, pl.ds(pl.multiple_of(at.low * 32, 32), 32)] + zb[k]
        energy = eb[0, 0:1, 0:1] + eb[k, 0:1, 0:1]
        denom = energy - vcol[own_rows, 0:1] - vir_ref[...]
        amplitude = summed / denom
        hi = amplitude.astype(jnp.bfloat16)
        am[k, 0, own_rows] = hi
        am[k, 1, own_rows] = (amplitude - hi.astype(jnp.float32)).astype(jnp.bfloat16)
        az_copy(k).start()

    def c5(k):
        az_copy(k).wait_recv()
        for n in range(3):
            ax_copy(k, n).start()
        ac_copy(k, 0).start()

    def c6(k):
        for n in range(3):
            ax_copy(k, n).wait_recv()
            ac_copy(k, (3, 1, 2)[n]).start()

    def c7(k):
        for n in range(4):
            ac_copy(k, n).wait_recv()
        hi, lo = pt[k, 0], pt[k, 1]
        out_ref[...] += dot_nt(hi, am[k, 0]) + dot_nt(hi, am[k, 1]) + dot_nt(lo, am[k, 0])
        energy = eb[0, 0:1, 0:1] + eb[k, 0:1, 0:1]
        total = jnp.zeros((1, 1), jnp.float32)
        for r in range(4):
            band = pl.ds(r * 128, 128)
            a = am[k, 0, band].astype(jnp.float32) + am[k, 1, band].astype(jnp.float32)
            b = am[k, 0, :, band].astype(jnp.float32) + am[k, 1, :, band].astype(jnp.float32)
            denom = energy - vcol[band, 0:1] - vir_ref[...]
            total += jnp.sum(a * denom * (2.0 * a - b.T), axis=(0, 1), keepdims=True)
        d = 0
        for place_of, distance in enumerate(ORDER):
            d += jnp.where(k == place_of, distance, 0)
        lane = lax.broadcasted_iota(jnp.int32, en_ref.shape, 1)
        en_ref[...] += jnp.where(lane == d, total / (512 * 512), 0.0)

    j_send((0, 0, None, "low"))
    for c in range(CHUNKS):
        f_copy(0, c).start()
        f_copy(1, c).start()
        if c < 2:
            f_spread(0, c)
    j_send((0, 0, None, 1), (0, 0, None, -1), (0, 0, None, "core"))
    fb[at.occ] = fit_ref[...]
    ib[at.fit] = int_ref[...]
    eb[0] = jnp.broadcast_to(occ_ref[...], (8, 128))
    out_ref[...] = jnp.zeros_like(out_ref)
    en_ref[...] = jnp.zeros_like(en_ref)
    vcol[...] = jnp.broadcast_to(vir_ref[...], (128, 512)).T
    for d in range(1, 6):
        energy_copy(d).start()

    def step(t, carry):
        @pl.when(t < CHUNKS)
        def _():
            f_first(t)

        @pl.when(t < 2)
        def _():
            f_spread(0, t + 2)

        @pl.when(t == 0)
        def _():
            j_relay(0)
            j_low()

        @pl.when((t >= 1) & (t <= CHUNKS))
        def _():
            f_second(t - 1)

        @pl.when(t == 1)
        def _():
            j_last(0)
            j_relay(1)

        @pl.when(t == 2)
        def _():
            j_last(1)
            j_core()
            fit_chunk(0)
            for d in range(1, 6):
                energy_copy(d).wait_recv()

        @pl.when((t >= 2) & (t <= CHUNKS))
        def _():
            fit_chunk(t - 1)

        for slot, first in ((SLOT[4], 3), (SLOT[1], 3), (SLOT[3], 4), (SLOT[2], 5)):
            c = t - first

            @pl.when((c >= 0) & (c < CHUNKS))
            def _():
                got(slot, c)
                send_on(slot, c)

        for slot, first in ((VIA, 3), (NEXT, 4)):
            c = t - first

            @pl.when((c >= 0) & (c < CHUNKS) & carries(y, c))
            def _():
                got(slot, c)
                send_on(slot, c)

        for j, stage in ((1, c2), (2, c3), (3, c4), (4, c5), (5, c6), (0, c1), (6, c7)):
            turn = t - 4 - j

            @pl.when((turn == 0) | ((turn >= 2) & (turn <= 6)))
            def _():
                stage(jnp.where(turn == 0, 0, turn - 1))

        return carry

    lax.fori_loop(0, 17, step, 0)

    for n in range(20):
        lax.fori_loop(0, CHUNKS, lambda c, _: (f_copy(n, c).wait_send(), _)[1], 0)
    for n in range(len(HOPS)):
        j_copy(n).wait_send()
    for n in range(len(ROUTES)):
        for c in range(CHUNKS):
            pl.when(takes(n, y, c))(lambda n=n, c=c: route(n, c).wait_send())
    for d in range(1, 6):
        energy_copy(d).wait_send()

    def finish(k, carry):
        core_copy(k).wait_send()
        z_copy(k).wait_send()
        az_copy(k).wait_send()
        for n in range(3):
            x_copy(k, n).wait_send()
            ax_copy(k, n).wait_send()
        for n in range(4):
            ac_copy(k, n).wait_send()
        return carry

    lax.fori_loop(0, 6, finish, 0)


def run(fitting, integrals, occ_energy, vir_energy):
    f32, bf16 = jnp.float32, jnp.bfloat16
    dma = pltpu.SemaphoreType.DMA
    return pl.pallas_call(
        kernel,
        out_shape=(
            jax.ShapeDtypeStruct((512, 512), f32),
            jax.ShapeDtypeStruct((8, 128), f32),
        ),
        in_specs=[pl.BlockSpec(memory_space=pltpu.VMEM)] * 4,
        out_specs=[pl.BlockSpec(memory_space=pltpu.VMEM)] * 2,
        scratch_shapes=[
            pltpu.VMEM((16, 512, 512), bf16),
            pltpu.VMEM((16, 512, 512), bf16),
            pltpu.VMEM((128, 512), f32),
            pltpu.VMEM((6, 2, 512, 512), bf16),
            pltpu.VMEM((2, 2, 256, 512), bf16),
            pltpu.VMEM((2, 512, 512), bf16),
            pltpu.VMEM((6, 256, 512), f32),
            pltpu.VMEM((6, 256, 512), f32),
            pltpu.VMEM((6, 256, 512), f32),
            pltpu.VMEM((6, 3, 64, 512), f32),
            pltpu.VMEM((6, 64, 512), f32),
            pltpu.VMEM((6, 32, 512), f32),
            pltpu.VMEM((6, 2, 512, 512), bf16),
            pltpu.VMEM((6, 8, 128), f32),
            pltpu.VMEM((512, 128), f32),
            dma((20, CHUNKS)), dma((16, CHUNKS, 2)),
            dma((17,)), dma((16, 2)),
            dma((len(ROUTES), CHUNKS)), dma((8, CHUNKS)),
            dma((6,)), dma((6,)),
            dma((6,)), dma((6,)),
            dma((6, 3)), dma((6, 3)),
            dma((6,)), dma((6,)),
            dma((6,)), dma((6,)),
            dma((6, 3)), dma((6, 3)),
            dma((6, 4)), dma((6, 4)),
        ],
        compiler_params=pltpu.CompilerParams(
            collective_id=0, has_side_effects=True, vmem_limit_bytes=60 * 1024 * 1024
        ),
    )(fitting, integrals, occ_energy, vir_energy)


def body(integrals, fitting, occ_energy, vir_energy):
    density, energies = run(fitting, integrals[:, 0, :], occ_energy[:, None], vir_energy[None, :])
    return (density[:, None, :], energies[0:1, 0:STOPS])


def solution(mesh):
    placed = (P("fit", "occ", None), P("fit", "occ"), P("occ"), P())
    return jax.shard_map(
        body,
        mesh=mesh,
        in_specs=placed,
        out_specs=(P("fit", "occ", None), P("occ", None)),
        check_vma=False,
    )
```

time: 255 us -> 254 us (level); the launches traced: 250 us -> 252 us
  Pallas kernels: 236 us -> 246 us
  local copies, waits for them, and re-layouts: 12.4 us -> 4.46 us
    pallas_call x2 -> x1, Pallas kernels: 236 us -> 246 us  [run(): pl.pallas_call(kernel, out_shape=(jax.ShapeDtypeStruct((512, 512), f32),...]
    another operation x1 -> x0, local copies, waits for them, and re-layouts: 3.93 us -> none  [body(): jnp.stack([energies[SLOT[d], 0] for d in range(STOPS)])[None, :]]
    unnamed x11 -> x1, local copies, waits for them, and re-layouts: 6.41 us -> 3.27 us
where the time goes in v3:
time: 254 us; the launch traced here: 252 us
  Pallas kernels  246 us (97%)
  local copies, waits for them, and re-layouts  4.46 us (2%)
    pallas_call x1, Pallas kernels, run(): pl.pallas_call(kernel, out_shape=(jax.ShapeDtypeStruct((512, 512), f32),...  246 us

profile of v3, /device:TPU:1, one launch (start us, length us, event | category | flops | bytes accessed | tf_op | source)
XLA Modules:
  0.0 251.6 jit_solution(6308576866022473638)
XLA Ops:
  1.3 245.9 %shard_map.59 = (f32[512,512]{1,0:T(8,128)}, f32[8,128]{1,0:T(8,128)}) custom-call(bf16[512,512]{1,0:T(8,128)(2,1)} %fit_ref.1, bf16[512,512]{1,0:T(8,128)(2,1)} %bitcast.6, f32[1,1]{1,0:T(1,128)} %bitcast.4.occ_ref, f32[1,512]{1,0:T(1,128)} %bitcast.7), custom_call_target="tpu_custom_call" | custom-call | tf_op jit(solution)/shard_map/pallas_call | solution.py:470
  247.2 3.3 %copy.6 = f32[512,1,512]{2,1,0:T(1,128)} copy(f32[512,1,512]{2,0,1:T(8,128)} %bitcast.5) | data formatting | bytes 2097152
  250.4 1.2 slice.3

commit v4 on v3

--- a/solution.py
+++ b/solution.py
@@ -52,24 +52,47 @@
     (NEXT, SLOT[5], 1, 0),
     (NEXT, SLOT[5], 0, -1),
 )
-HOPS = (
-    (0, 0, None, "low"),
-    (0, 0, None, 1),
-    (0, 0, None, -1),
-    (0, 0, None, "core"),
-    (0, 1, None, 1),
-    (0, 1, None, -1),
-    (0, 1, None, "core"),
-    (1, 0, 0, -1),
-    (1, 0, None, "core"),
-    (-1, 0, 1, 1),
-    (-1, 0, None, "core"),
-    (1, 1, 0, -1),
-    (1, 1, None, "core"),
-    (-1, 1, 1, 1),
-    (-1, 1, None, "core"),
-    (2, 0, None, "core"),
-    (2, 1, None, "core"),
+HOPS = tuple((0, 0, h, to) for h in (0, 1) for to in ("low", 1, -1)) + tuple(
+    (0, 1, h, to) for h in (0, 1) for to in (1, -1)
+) + ((0, 0, None, "core"), (0, 1, None, "core")) + tuple(
+    hop
+    for low in (0, 1)
+    for hop in (
+        (1, low, 0, -1),
+        (-1, low, 1, 1),
+        (1, low, None, "core"),
+        (-1, low, None, "core"),
+        (2, low, None, "core"),
+    )
+)
+PLAN = (
+    ("oz", 0), ("oy", 2), ("jl", 0), ("jl", 1), ("oz", 1), ("jo",), ("oy", 3), ("oz", 2), ("oy", 0),
+    ("jr", 0, 0), ("a3", 0), ("a1", 0), ("oy", 1), ("b", 0, 3), ("b", 3, 0), ("b", 1, 0), ("oz", 3),
+    ("jg", 0), ("b", 0, 0), ("a1", 1), ("jg", 1), ("a3", 1), ("a1", 3), ("jr", 0, 1), ("a3", 2),
+    ("jt", 0), ("jr", 1, 0), ("jr", 1, 1), ("a2", 0), ("b", 1, 1), ("jt", 1), ("b", 0, 1),
+    ("b", 2, 0), ("a1", 2), ("b", 3, 1), ("f1", 0), ("a2", 1), ("f2", 0), ("b", 3, 2), ("a2", 2),
+    ("b", 2, 1), ("a3", 3), ("b", 0, 2), ("b", 1, 2), ("f1", 1), ("b", 2, 2), ("f2", 1), ("a2", 3),
+    ("f1", 2), ("b", 1, 3), ("b", 3, 3), ("f2", 2), ("b", 2, 3), ("py", 0), ("g", 4, 0, 1),
+    ("g", 4, 0, 0), ("f1", 3), ("py", 1), ("g", 4, 1, 1), ("f2", 3), ("g", 4, 0, 2), ("g", 4, 1, 0),
+    ("c", 1, 0), ("py", 2), ("c", 2, 0), ("g", "V", 2, 0), ("g", 3, 0, 0), ("g", 3, 0, 1),
+    ("g", 4, 2, 1), ("g", 3, 1, 1), ("g", 3, 0, 2), ("g", 3, 1, 2), ("g", 1, 0, 3), ("py", 3),
+    ("g", "V", 0, 3), ("g", 4, 2, 3), ("c", 3, 0), ("c", 4, 0), ("g", 4, 2, 0), ("g", 4, 0, 3),
+    ("g", 4, 1, 2), ("g", 1, 0, 0), ("g", 2, 0, 3), ("g", 3, 1, 0), ("g", 4, 2, 2), ("g", 4, 1, 3),
+    ("g", 1, 1, 1), ("g", "V", 3, 0), ("g", 1, 0, 2), ("g", 1, 0, 1), ("g", 4, 3, 3), ("c", 5, 0),
+    ("g", 1, 2, 2), ("g", 1, 1, 3), ("g", 4, 3, 0), ("g", "V", 1, 3), ("g", 1, 1, 2),
+    ("g", 1, 3, 2), ("g", 4, 3, 1), ("g", 1, 1, 0), ("g", 4, 3, 2), ("g", 1, 2, 0), ("c", 1, 1),
+    ("c", 2, 1), ("g", "N", 0, 3), ("g", 3, 1, 3), ("g", 1, 3, 0), ("g", 1, 3, 3), ("g", 3, 3, 0),
+    ("g", 2, 1, 3), ("g", 3, 0, 3), ("g", 2, 0, 2), ("g", 1, 2, 1), ("g", 3, 2, 3), ("g", 3, 2, 2),
+    ("g", 1, 2, 3), ("g", 1, 3, 1), ("g", 3, 2, 0), ("g", 3, 2, 1), ("g", 2, 1, 2), ("c", 1, 2),
+    ("c", 2, 2), ("g", 3, 3, 1), ("g", 3, 3, 3), ("g", 3, 3, 2), ("c", 1, 3), ("c", 3, 1),
+    ("c", 2, 3), ("g", 2, 0, 0), ("g", 2, 0, 1), ("g", 2, 1, 1), ("g", 2, 2, 3), ("c", 4, 1),
+    ("c", 3, 2), ("g", 2, 1, 0), ("g", 2, 3, 1), ("c", 5, 1), ("g", "N", 1, 3), ("g", 2, 2, 0),
+    ("g", "N", 3, 0), ("g", 2, 3, 2), ("c", 3, 3), ("g", 2, 2, 2), ("g", 2, 3, 0), ("g", 2, 3, 3),
+    ("c", 6, 0), ("c", 4, 2), ("g", "N", 2, 0), ("g", 2, 2, 1), ("c", 1, 4), ("c", 2, 4),
+    ("c", 4, 3), ("c", 5, 3), ("c", 3, 4), ("c", 1, 5), ("c", 2, 5), ("c", 5, 2), ("c", 6, 1),
+    ("c", 6, 3), ("c", 7, 0), ("c", 4, 4), ("c", 7, 1), ("c", 3, 5), ("c", 5, 4), ("c", 6, 2),
+    ("c", 4, 5), ("c", 7, 3), ("c", 5, 5), ("c", 6, 4), ("c", 7, 2), ("c", 7, 4), ("c", 6, 5),
+    ("c", 7, 5),
 )
 
 
@@ -159,22 +182,20 @@
         f_copy(4 + 2 * dz, c).start()
         f_copy(5 + 2 * dz, c).start()
 
-    def f_first(c):
-        f_got(1, 0, c)
-        f_copy(2, c).start()
-        f_spread(1, c)
-        f_got(3, 0, c)
-        f_copy(3, c).start()
-        f_spread(3, c)
+    def f_near(dz, c):
+        f_got(dz, 0, c)
+        f_copy(2 if dz == 1 else 3, c).start()
+        f_spread(dz, c)
+
+    def f_far(c):
         f_got(2, 0, c)
         f_spread(2, c)
 
-    def f_second(c):
-        for dz in (0, 1, 3, 2):
-            f_got(dz, 1, c)
-            f_copy(12 + 2 * dz, c).start()
-            f_got(dz, 3, c)
-            f_copy(13 + 2 * dz, c).start()
+    def f_side(dz, c):
+        f_got(dz, 1, c)
+        f_got(dz, 3, c)
+        f_copy(12 + 2 * dz, c).start()
+        f_copy(13 + 2 * dz, c).start()
 
     def j_copy(n):
         dx, flip_low, half, to = HOPS[n]
@@ -188,29 +209,39 @@
         for hop in hops:
             j_copy(HOPS.index(hop)).start()
 
-    def j_got(slot, halves):
-        for half in (0, 1) if halves else (None,):
-            where = pl.ds(0, 512) if half is None else pl.ds(half * 256, 256)
-            part = ib.at[slot, where]
-            remote(part, part, js.at[0], jr.at[slot, half or 0], at.occ, at.fit).wait_recv()
-
-    def j_relay(flip_low):
-        for dx, half in ((1, 0), (-1, 1)):
-            j_got(at.f(dx, flip_low), False)
-            j_send((dx, flip_low, half, -dx), (dx, flip_low, None, "core"))
-
-    def j_last(flip_low):
-        j_got(at.f(2, flip_low), True)
-        j_send((2, flip_low, None, "core"))
-
-    def j_low():
-        j_got(at.f(0, 1), False)
-        j_send((0, 1, None, 1), (0, 1, None, -1), (0, 1, None, "core"))
+    def j_got(slot, half):
+        where = pl.ds(0, 512) if half is None else pl.ds(half * 256, 256)
+        part = ib.at[slot, where]
+        remote(part, part, js.at[0], jr.at[slot, half or 0], at.occ, at.fit).wait_recv()
+
+    def j_own():
+        for h in (0, 1):
+            j_send((0, 0, h, -1), (0, 0, 1 - h, 1))
+        j_send((0, 0, None, "core"))
+
+    def j_low(h):
+        j_got(at.f(0, 1), h)
+        j_send((0, 1, h, -1), (0, 1, h, 1))
+        if h == 1:
+            j_send((0, 1, None, "core"))
+
+    def j_relay(second, low):
+        j_got(at.f(1, low), second)
+        j_got(at.f(-1, low), 1 - second)
+        if second:
+            j_send((1, low, None, "core"), (-1, low, None, "core"))
+        else:
+            j_send((1, low, 0, -1), (-1, low, 1, 1))
+
+    def j_last(low):
+        j_got(at.f(2, low), 0)
+        j_got(at.f(2, low), 1)
+        j_send((2, low, None, "core"))
 
     def j_core():
-        for flip_low in (0, 1):
+        for low in (0, 1):
             for dx in (0, 1, -1, 2):
-                j_got(at.f(dx, flip_low, 1), False)
+                j_got(at.f(dx, low, 1), None)
 
     def place(slot, c):
         if slot >= VIA:
@@ -221,9 +252,9 @@
         src, dst, dz, dy = ROUTES[n]
         return remote(place(src, c), place(dst, c), rs.at[n, c], rr.at[dst, c], at.o(dz, dy), at.fit)
 
-    def send_on(slot, c):
-        for n in range(len(ROUTES)):
-            if ROUTES[n][0] == slot:
+    def send_on(slot, c, over_z=None):
+        for n, (source, _, dz, _) in enumerate(ROUTES):
+            if source == slot and over_z in (None, dz != 0):
                 pl.when(takes(n, y, c))(lambda n=n: route(n, c).start())
 
     def got(slot, c):
@@ -234,21 +265,25 @@
         k = SLOT[d]
         return remote(eb.at[0], eb.at[k], es.at[k], er.at[k], behind[d - 1], at.fit)
 
-    def fit_chunk(c):
-        def add(dy):
-            def one(dz, carry):
-                slot = at.o(dz, dy)
-                acc[...] += dot_nn(fb[slot, rows(c)], ib[slot])
-                return carry
-
-            lax.fori_loop(0, 4, one, 0)
-
+    def add(dy, c):
+        def one(dz, carry):
+            slot = at.o(dz, dy)
+            acc[...] += dot_nn(fb[slot, rows(c)], ib[slot])
+            return carry
+
+        lax.fori_loop(0, 4, one, 0)
+
+    def fit_most(c):
+        if c == 0:
+            j_core()
         acc[...] = jnp.zeros_like(acc)
         for dy in (0, 1, 3):
-            add(dy)
+            add(dy, c)
+
+    def fit_rest(c):
         for dz in range(4):
             f_got(dz, 2, c)
-        add(2)
+        add(2, c)
         whole = acc[...]
         hi = whole.astype(jnp.bfloat16)
         low = whole - hi.astype(jnp.float32)
@@ -256,7 +291,7 @@
         pt[0, 1, rows(c)] = low.astype(jnp.bfloat16)
         ownt[0, :, rows(c)] = hi.astype(jnp.float32).T.astype(jnp.bfloat16)
         ownt[1, :, rows(c)] = low.T.astype(jnp.bfloat16)
-        send_on(0, c)
+        send_on(0, c, True)
 
     mine = pl.ds(pl.multiple_of(at.core * 256, 256), 256)
     other = pl.ds(pl.multiple_of((1 - at.core) * 256, 256), 256)
@@ -293,8 +328,7 @@
         return remote(part, part, acs.at[k, n], acr.at[k, n], at.occ, core_peer)
 
     def c1(k):
-        @pl.when(k == 5)
-        def _():
+        if k == 5:
             for c in range(CHUNKS):
                 got(SLOT[5], c)
 
@@ -356,89 +390,61 @@
             b = am[k, 0, :, band].astype(jnp.float32) + am[k, 1, :, band].astype(jnp.float32)
             denom = energy - vcol[band, 0:1] - vir_ref[...]
             total += jnp.sum(a * denom * (2.0 * a - b.T), axis=(0, 1), keepdims=True)
-        d = 0
-        for place_of, distance in enumerate(ORDER):
-            d += jnp.where(k == place_of, distance, 0)
         lane = lax.broadcasted_iota(jnp.int32, en_ref.shape, 1)
-        en_ref[...] += jnp.where(lane == d, total / (512 * 512), 0.0)
-
-    j_send((0, 0, None, "low"))
-    for c in range(CHUNKS):
+        en_ref[...] += jnp.where(lane == ORDER[k], total / (512 * 512), 0.0)
+
+    def fill():
+        fb[at.occ] = fit_ref[...]
+        ib[at.fit] = int_ref[...]
+        eb[0] = jnp.broadcast_to(occ_ref[...], (8, 128))
+        out_ref[...] = jnp.zeros_like(out_ref)
+        en_ref[...] = jnp.zeros_like(en_ref)
+        vcol[...] = jnp.broadcast_to(vir_ref[...], (128, 512)).T
+        for d in range(1, 6):
+            energy_copy(d).start()
+
+    def relay(d, c, only):
+        slot = SLOT.get(d, {"V": VIA, "N": NEXT}.get(d))
+
+        @pl.when(y == only)
+        def _():
+            got(slot, c)
+            for n in range(len(ROUTES)):
+                if ROUTES[n][0] == slot and takes(n, only, c):
+                    route(n, c).start()
+
+    def own_z(c):
         f_copy(0, c).start()
         f_copy(1, c).start()
-        if c < 2:
-            f_spread(0, c)
-    j_send((0, 0, None, 1), (0, 0, None, -1), (0, 0, None, "core"))
-    fb[at.occ] = fit_ref[...]
-    ib[at.fit] = int_ref[...]
-    eb[0] = jnp.broadcast_to(occ_ref[...], (8, 128))
-    out_ref[...] = jnp.zeros_like(out_ref)
-    en_ref[...] = jnp.zeros_like(en_ref)
-    vcol[...] = jnp.broadcast_to(vir_ref[...], (128, 512)).T
-    for d in range(1, 6):
-        energy_copy(d).start()
-
-    def step(t, carry):
-        @pl.when(t < CHUNKS)
-        def _():
-            f_first(t)
-
-        @pl.when(t < 2)
-        def _():
-            f_spread(0, t + 2)
-
-        @pl.when(t == 0)
-        def _():
-            j_relay(0)
-            j_low()
-
-        @pl.when((t >= 1) & (t <= CHUNKS))
-        def _():
-            f_second(t - 1)
-
-        @pl.when(t == 1)
-        def _():
-            j_last(0)
-            j_relay(1)
-
-        @pl.when(t == 2)
-        def _():
-            j_last(1)
-            j_core()
-            fit_chunk(0)
+
+    stages = {1: c1, 2: c2, 3: c3, 4: c4, 5: c5, 6: c6, 7: c7}
+    steps = {
+        "oz": own_z,
+        "oy": lambda c: f_spread(0, c),
+        "a1": lambda c: f_near(1, c),
+        "a3": lambda c: f_near(3, c),
+        "a2": f_far,
+        "b": f_side,
+        "jl": lambda h: j_send((0, 0, h, "low")),
+        "jo": j_own,
+        "jg": j_low,
+        "jr": j_relay,
+        "jt": j_last,
+        "f1": fit_most,
+        "f2": fit_rest,
+        "py": lambda c: send_on(0, c, False),
+        "g": relay,
+        "c": lambda j, k: stages[j](k),
+    }
+    filled = False
+    for name, *rest in PLAN:
+        if not filled and name not in ("oz", "oy", "jl", "jo"):
+            fill()
+            filled = True
+        if (name, *rest) == ("f2", 3):
             for d in range(1, 6):
                 energy_copy(d).wait_recv()
-
-        @pl.when((t >= 2) & (t <= CHUNKS))
-        def _():
-            fit_chunk(t - 1)
-
-        for slot, first in ((SLOT[4], 3), (SLOT[1], 3), (SLOT[3], 4), (SLOT[2], 5)):
-            c = t - first
-
-            @pl.when((c >= 0) & (c < CHUNKS))
-            def _():
-                got(slot, c)
-                send_on(slot, c)
-
-        for slot, first in ((VIA, 3), (NEXT, 4)):
-            c = t - first
-
-            @pl.when((c >= 0) & (c < CHUNKS) & carries(y, c))
-            def _():
-                got(slot, c)
-                send_on(slot, c)
-
-        for j, stage in ((1, c2), (2, c3), (3, c4), (4, c5), (5, c6), (0, c1), (6, c7)):
-            turn = t - 4 - j
-
-            @pl.when((turn == 0) | ((turn >= 2) & (turn <= 6)))
-            def _():
-                stage(jnp.where(turn == 0, 0, turn - 1))
-
-        return carry
-
-    lax.fori_loop(0, 17, step, 0)
+        steps[name](*rest)
 
     for n in range(20):
         lax.fori_loop(0, CHUNKS, lambda c, _: (f_copy(n, c).wait_send(), _)[1], 0)
@@ -492,7 +498,7 @@
             pltpu.VMEM((6, 8, 128), f32),
             pltpu.VMEM((512, 128), f32),
             dma((20, CHUNKS)), dma((16, CHUNKS, 2)),
-            dma((17,)), dma((16, 2)),
+            dma((len(HOPS),)), dma((16, 2)),
             dma((len(ROUTES), CHUNKS)), dma((8, CHUNKS)),
             dma((6,)), dma((6,)),
             dma((6,)), dma((6,)),

time: 254 us -> 207 us (0.81)
  Pallas kernels: 246 us -> 201 us
    pallas_call x1, Pallas kernels: 246 us -> 201 us  [run(): pl.pallas_call(kernel, out_shape=(jax.ShapeDtypeStruct((512, 512), f32),...]
where the time goes in v4:
time: 207 us
  Pallas kernels  201 us (97%)
  local copies, waits for them, and re-layouts  4.46 us (2%)
    pallas_call x1, Pallas kernels, run(): pl.pallas_call(kernel, out_shape=(jax.ShapeDtypeStruct((512, 512), f32),...  201 us

profile of v4, /device:TPU:1, one launch (start us, length us, event | category | flops | bytes accessed | tf_op | source)
XLA Modules:
  0.0 206.5 jit_solution(9190873376261173414)
XLA Ops:
  1.3 200.8 %shard_map.59 = (f32[512,512]{1,0:T(8,128)}, f32[8,128]{1,0:T(8,128)}) custom-call(bf16[512,512]{1,0:T(8,128)(2,1)} %fit_ref.1, bf16[512,512]{1,0:T(8,128)(2,1)} %bitcast.6, f32[1,1]{1,0:T(1,128)} %bitcast.4.occ_ref, f32[1,512]{1,0:T(1,128)} %bitcast.7), custom_call_target="tpu_custom_call" | custom-call | tf_op jit(solution)/shard_map/pallas_call | solution.py:476
  202.1 3.3 %copy.6 = f32[512,1,512]{2,1,0:T(1,128)} copy(f32[512,1,512]{2,0,1:T(8,128)} %bitcast.5) | data formatting | bytes 2097152
  205.3 1.2 slice.3

commit v5 on v4

--- a/solution.py
+++ b/solution.py
@@ -65,34 +65,35 @@
         (2, low, None, "core"),
     )
 )
+LOW_FIRST = (2, 4)
 PLAN = (
-    ("oz", 0), ("oy", 2), ("jl", 0), ("jl", 1), ("oz", 1), ("jo",), ("oy", 3), ("oz", 2), ("oy", 0),
-    ("jr", 0, 0), ("a3", 0), ("a1", 0), ("oy", 1), ("b", 0, 3), ("b", 3, 0), ("b", 1, 0), ("oz", 3),
-    ("jg", 0), ("b", 0, 0), ("a1", 1), ("jg", 1), ("a3", 1), ("a1", 3), ("jr", 0, 1), ("a3", 2),
-    ("jt", 0), ("jr", 1, 0), ("jr", 1, 1), ("a2", 0), ("b", 1, 1), ("jt", 1), ("b", 0, 1),
-    ("b", 2, 0), ("a1", 2), ("b", 3, 1), ("f1", 0), ("a2", 1), ("f2", 0), ("b", 3, 2), ("a2", 2),
-    ("b", 2, 1), ("a3", 3), ("b", 0, 2), ("b", 1, 2), ("f1", 1), ("b", 2, 2), ("f2", 1), ("a2", 3),
-    ("f1", 2), ("b", 1, 3), ("b", 3, 3), ("f2", 2), ("b", 2, 3), ("py", 0), ("g", 4, 0, 1),
-    ("g", 4, 0, 0), ("f1", 3), ("py", 1), ("g", 4, 1, 1), ("f2", 3), ("g", 4, 0, 2), ("g", 4, 1, 0),
-    ("c", 1, 0), ("py", 2), ("c", 2, 0), ("g", "V", 2, 0), ("g", 3, 0, 0), ("g", 3, 0, 1),
-    ("g", 4, 2, 1), ("g", 3, 1, 1), ("g", 3, 0, 2), ("g", 3, 1, 2), ("g", 1, 0, 3), ("py", 3),
-    ("g", "V", 0, 3), ("g", 4, 2, 3), ("c", 3, 0), ("c", 4, 0), ("g", 4, 2, 0), ("g", 4, 0, 3),
-    ("g", 4, 1, 2), ("g", 1, 0, 0), ("g", 2, 0, 3), ("g", 3, 1, 0), ("g", 4, 2, 2), ("g", 4, 1, 3),
-    ("g", 1, 1, 1), ("g", "V", 3, 0), ("g", 1, 0, 2), ("g", 1, 0, 1), ("g", 4, 3, 3), ("c", 5, 0),
-    ("g", 1, 2, 2), ("g", 1, 1, 3), ("g", 4, 3, 0), ("g", "V", 1, 3), ("g", 1, 1, 2),
-    ("g", 1, 3, 2), ("g", 4, 3, 1), ("g", 1, 1, 0), ("g", 4, 3, 2), ("g", 1, 2, 0), ("c", 1, 1),
-    ("c", 2, 1), ("g", "N", 0, 3), ("g", 3, 1, 3), ("g", 1, 3, 0), ("g", 1, 3, 3), ("g", 3, 3, 0),
-    ("g", 2, 1, 3), ("g", 3, 0, 3), ("g", 2, 0, 2), ("g", 1, 2, 1), ("g", 3, 2, 3), ("g", 3, 2, 2),
-    ("g", 1, 2, 3), ("g", 1, 3, 1), ("g", 3, 2, 0), ("g", 3, 2, 1), ("g", 2, 1, 2), ("c", 1, 2),
-    ("c", 2, 2), ("g", 3, 3, 1), ("g", 3, 3, 3), ("g", 3, 3, 2), ("c", 1, 3), ("c", 3, 1),
-    ("c", 2, 3), ("g", 2, 0, 0), ("g", 2, 0, 1), ("g", 2, 1, 1), ("g", 2, 2, 3), ("c", 4, 1),
-    ("c", 3, 2), ("g", 2, 1, 0), ("g", 2, 3, 1), ("c", 5, 1), ("g", "N", 1, 3), ("g", 2, 2, 0),
-    ("g", "N", 3, 0), ("g", 2, 3, 2), ("c", 3, 3), ("g", 2, 2, 2), ("g", 2, 3, 0), ("g", 2, 3, 3),
-    ("c", 6, 0), ("c", 4, 2), ("g", "N", 2, 0), ("g", 2, 2, 1), ("c", 1, 4), ("c", 2, 4),
-    ("c", 4, 3), ("c", 5, 3), ("c", 3, 4), ("c", 1, 5), ("c", 2, 5), ("c", 5, 2), ("c", 6, 1),
-    ("c", 6, 3), ("c", 7, 0), ("c", 4, 4), ("c", 7, 1), ("c", 3, 5), ("c", 5, 4), ("c", 6, 2),
-    ("c", 4, 5), ("c", 7, 3), ("c", 5, 5), ("c", 6, 4), ("c", 7, 2), ("c", 7, 4), ("c", 6, 5),
-    ("c", 7, 5),
+    ("oy", 0), ("oz", 0), ("oy", 2), ("jo",), ("oy", 3), ("oy", 1), ("jl", 0), ("jl", 1), ("oz", 1),
+    ("oz", 2), ("a3", 0), ("jr", 0, 0), ("b", 0, 3), ("jr", 1, 0), ("oz", 3), ("b", 0, 1),
+    ("jg", 0), ("b", 3, 0), ("a1", 1), ("b", 0, 0), ("a1", 0), ("jg", 1), ("a3", 1), ("a1", 3),
+    ("jr", 0, 1), ("jt", 0), ("a3", 2), ("jr", 1, 1), ("a2", 0), ("b", 1, 1), ("b", 1, 0),
+    ("jt", 1), ("b", 2, 0), ("b", 3, 1), ("a1", 2), ("f1", 0), ("a2", 1), ("f2", 0), ("a2", 2),
+    ("b", 2, 1), ("b", 0, 2), ("a3", 3), ("b", 3, 2), ("b", 1, 2), ("f1", 1), ("b", 2, 2),
+    ("f2", 1), ("a2", 3), ("b", 1, 3), ("f1", 2), ("b", 3, 3), ("f2", 2), ("b", 2, 3), ("py", 0),
+    ("g", 4, 0, 1), ("py", 1), ("py", 2), ("g", 4, 0, 0), ("g", 4, 0, 2), ("g", "V", 0, 3),
+    ("f1", 3), ("g", 4, 1, 1), ("f2", 3), ("c", 1, 0), ("py", 3), ("g", "V", 1, 3), ("g", 4, 1, 0),
+    ("g", 3, 0, 0), ("c", 2, 0), ("g", 4, 2, 3), ("g", 4, 2, 0), ("g", 1, 0, 1), ("g", "N", 0, 3),
+    ("g", 3, 0, 1), ("g", 3, 1, 0), ("g", 1, 1, 0), ("g", 2, 0, 3), ("g", 3, 1, 1), ("g", 1, 1, 1),
+    ("g", 4, 2, 1), ("g", 4, 1, 2), ("c", 3, 0), ("g", 3, 0, 2), ("g", 2, 0, 2), ("g", 3, 0, 3),
+    ("c", 4, 0), ("g", "V", 2, 0), ("g", 4, 1, 3), ("g", 4, 2, 2), ("g", 4, 3, 3), ("g", 4, 3, 0),
+    ("g", 4, 3, 2), ("g", 4, 0, 3), ("g", 4, 3, 1), ("c", 1, 1), ("g", 1, 0, 3), ("g", 2, 1, 2),
+    ("g", 2, 0, 0), ("g", 3, 2, 1), ("c", 2, 1), ("g", "V", 3, 0), ("g", 1, 2, 1), ("g", 1, 2, 0),
+    ("g", 1, 1, 2), ("g", 1, 0, 0), ("g", 3, 1, 2), ("g", 3, 2, 3), ("g", 3, 3, 0), ("c", 5, 0),
+    ("g", 3, 1, 3), ("g", 2, 1, 1), ("g", 1, 2, 3), ("g", 3, 3, 3), ("g", 1, 3, 1),
+    ("g", "N", 1, 3), ("g", 1, 2, 2), ("g", 1, 0, 2), ("g", 1, 3, 0), ("g", 3, 2, 2),
+    ("g", 1, 3, 3), ("g", 1, 3, 2), ("g", 3, 2, 0), ("g", 1, 1, 3), ("c", 1, 2), ("g", 3, 3, 1),
+    ("g", 3, 3, 2), ("c", 1, 3), ("c", 3, 1), ("c", 2, 2), ("g", 2, 1, 3), ("c", 2, 3),
+    ("g", 2, 3, 1), ("g", 2, 2, 2), ("c", 4, 1), ("g", "N", 2, 0), ("g", 2, 2, 1), ("g", 2, 2, 0),
+    ("g", 2, 0, 1), ("g", "N", 3, 0), ("g", 2, 3, 0), ("g", 2, 2, 3), ("c", 3, 2), ("g", 2, 3, 2),
+    ("g", 2, 3, 3), ("g", 2, 1, 0), ("c", 1, 4), ("c", 5, 1), ("c", 3, 3), ("c", 2, 4), ("c", 4, 2),
+    ("c", 4, 3), ("c", 1, 5), ("c", 3, 4), ("c", 2, 5), ("c", 6, 1), ("c", 6, 0), ("c", 5, 2),
+    ("c", 4, 4), ("c", 5, 3), ("c", 7, 1), ("c", 6, 2), ("c", 3, 5), ("c", 4, 5), ("c", 5, 4),
+    ("c", 5, 5), ("c", 7, 2), ("c", 6, 3), ("c", 7, 0), ("c", 6, 4), ("c", 7, 3), ("c", 6, 5),
+    ("c", 7, 4), ("c", 7, 5),
 )
 
 
@@ -129,7 +130,7 @@
 
 def kernel(
     fit_ref, int_ref, occ_ref, vir_ref, out_ref, en_ref,
-    fb, ib, acc, pt, spare, ownt, pbo, hb, cb, xb, qb, zb, am, eb, vcol,
+    fb, ib, acc, pt, spare, ownt, pbo, hb, cb, xb, qb, zb, qz, zz, am, eb, vcol,
     fs, fr, js, jr, rs, rr, es, er, cs, cr, xs, xr, zs, zr, azs, azr, axs, axr, acs, acr,
 ):
     at = Place()
@@ -304,27 +305,52 @@
 
     def x_copy(k, n):
         to = (at.x + (1, 3, 2)[n]) % 4
-        return remote(hb.at[k, quarter(to)], xb.at[k, n], xs.at[k, n], xr.at[k, n], at.occ, x_peers[n])
+        if k in LOW_FIRST:
+            src, dst = qz.at[k, pl.ds(pl.multiple_of(to * 32, 32), 32)], xb.at[k, n, pl.ds(0, 32)]
+        else:
+            src, dst = hb.at[k, quarter(to)], xb.at[k, n]
+        return remote(src, dst, xs.at[k, n], xr.at[k, n], at.occ, x_peers[n])
+
+    def half_of(low):
+        return pl.ds(pl.multiple_of(low * 128, 128), 128)
 
     def z_copy(k):
-        half = pl.ds(pl.multiple_of((1 - at.low) * 32, 32), 32)
-        return remote(qb.at[k, half], zb.at[k], zs.at[k], zr.at[k], at.occ, low_peer)
+        if k in LOW_FIRST:
+            src, dst = hb.at[k, half_of(1 - at.low)], zz.at[k]
+        else:
+            half = pl.ds(pl.multiple_of((1 - at.low) * 32, 32), 32)
+            src, dst = qb.at[k, half], zb.at[k]
+        return remote(src, dst, zs.at[k], zr.at[k], at.occ, low_peer)
 
     def block(x, core):
         return pl.ds(pl.multiple_of(core * 256 + x * 64, 64), 64)
 
-    own_rows = pl.ds(pl.multiple_of(at.core * 256 + at.x * 64 + at.low * 32, 32), 32)
+    def own_rows(k):
+        if k in LOW_FIRST:
+            start = at.core * 256 + at.low * 128 + at.x * 32
+        else:
+            start = at.core * 256 + at.x * 64 + at.low * 32
+        return pl.ds(pl.multiple_of(start, 32), 32)
+
+    def low_rows(low):
+        return pl.ds(pl.multiple_of(at.core * 256 + low * 128, 128), 128)
 
     def az_copy(k):
-        part = am.at[k, :, own_rows]
+        part = am.at[k, :, low_rows(at.low) if k in LOW_FIRST else own_rows(k)]
         return remote(part, part, azs.at[k], azr.at[k], at.occ, low_peer)
 
     def ax_copy(k, n):
-        part = am.at[k, :, block(at.x, at.core)]
+        part = am.at[k, :, own_rows(k) if k in LOW_FIRST else block(at.x, at.core)]
         return remote(part, part, axs.at[k, n], axr.at[k, n], at.occ, x_peers[n])
 
+    def ac_parts(k):
+        return 2 if k in LOW_FIRST else 4
+
     def ac_copy(k, n):
-        part = am.at[k, :, block((at.x + n) % 4, at.core)]
+        if k in LOW_FIRST:
+            part = am.at[k, :, low_rows(at.low if n == 0 else 1 - at.low)]
+        else:
+            part = am.at[k, :, block((at.x + n) % 4, at.core)]
         return remote(part, part, acs.at[k, n], acr.at[k, n], at.occ, core_peer)
 
     def c1(k):
@@ -343,42 +369,71 @@
         core_copy(k).start()
         hb[k] = part(mine)
 
+    def start_x(copy, k):
+        for n in range(3):
+            copy(k, n).start()
+
+    def wait_x(copy, k):
+        for n in range(3):
+            copy(k, n).wait_recv()
+
     def c2(k):
         core_copy(k).wait_recv()
         hb[k] += cb[k]
-        for n in range(3):
-            x_copy(k, n).start()
+        if k in LOW_FIRST:
+            z_copy(k).start()
+        else:
+            start_x(x_copy, k)
 
     def c3(k):
-        for n in range(3):
-            x_copy(k, n).wait_recv()
-        qb[k] = (hb[k, quarter(at.x)] + xb[k, 0]) + (xb[k, 1] + xb[k, 2])
-        z_copy(k).start()
+        if k in LOW_FIRST:
+            z_copy(k).wait_recv()
+            qz[k] = hb[k, half_of(at.low)] + zz[k]
+            start_x(x_copy, k)
+        else:
+            wait_x(x_copy, k)
+            qb[k] = (hb[k, quarter(at.x)] + xb[k, 0]) + (xb[k, 1] + xb[k, 2])
+            z_copy(k).start()
 
     def c4(k):
-        z_copy(k).wait_recv()
-        summed = qb[k, pl.ds(pl.multiple_of(at.low * 32, 32), 32)] + zb[k]
+        if k in LOW_FIRST:
+            wait_x(x_copy, k)
+            own = qz[k, pl.ds(pl.multiple_of(at.x * 32, 32), 32)]
+            summed = (own + xb[k, 0, 0:32]) + (xb[k, 1, 0:32] + xb[k, 2, 0:32])
+        else:
+            z_copy(k).wait_recv()
+            summed = qb[k, pl.ds(pl.multiple_of(at.low * 32, 32), 32)] + zb[k]
         energy = eb[0, 0:1, 0:1] + eb[k, 0:1, 0:1]
-        denom = energy - vcol[own_rows, 0:1] - vir_ref[...]
+        denom = energy - vcol[own_rows(k), 0:1] - vir_ref[...]
         amplitude = summed / denom
         hi = amplitude.astype(jnp.bfloat16)
-        am[k, 0, own_rows] = hi
-        am[k, 1, own_rows] = (amplitude - hi.astype(jnp.float32)).astype(jnp.bfloat16)
-        az_copy(k).start()
+        am[k, 0, own_rows(k)] = hi
+        am[k, 1, own_rows(k)] = (amplitude - hi.astype(jnp.float32)).astype(jnp.bfloat16)
+        if k in LOW_FIRST:
+            start_x(ax_copy, k)
+        else:
+            az_copy(k).start()
 
     def c5(k):
-        az_copy(k).wait_recv()
-        for n in range(3):
-            ax_copy(k, n).start()
+        if k in LOW_FIRST:
+            wait_x(ax_copy, k)
+            az_copy(k).start()
+        else:
+            az_copy(k).wait_recv()
+            start_x(ax_copy, k)
         ac_copy(k, 0).start()
 
     def c6(k):
-        for n in range(3):
-            ax_copy(k, n).wait_recv()
-            ac_copy(k, (3, 1, 2)[n]).start()
+        if k in LOW_FIRST:
+            az_copy(k).wait_recv()
+            ac_copy(k, 1).start()
+        else:
+            for n in range(3):
+                ax_copy(k, n).wait_recv()
+                ac_copy(k, (3, 1, 2)[n]).start()
 
     def c7(k):
-        for n in range(4):
+        for n in range(ac_parts(k)):
             ac_copy(k, n).wait_recv()
         hi, lo = pt[k, 0], pt[k, 1]
         out_ref[...] += dot_nt(hi, am[k, 0]) + dot_nt(hi, am[k, 1]) + dot_nt(lo, am[k, 0])
@@ -456,18 +511,15 @@
     for d in range(1, 6):
         energy_copy(d).wait_send()
 
-    def finish(k, carry):
+    for k in range(6):
         core_copy(k).wait_send()
         z_copy(k).wait_send()
         az_copy(k).wait_send()
         for n in range(3):
             x_copy(k, n).wait_send()
             ax_copy(k, n).wait_send()
-        for n in range(4):
+        for n in range(ac_parts(k)):
             ac_copy(k, n).wait_send()
-        return carry
-
-    lax.fori_loop(0, 6, finish, 0)
 
 
 def run(fitting, integrals, occ_energy, vir_energy):
@@ -494,6 +546,8 @@
             pltpu.VMEM((6, 3, 64, 512), f32),
             pltpu.VMEM((6, 64, 512), f32),
             pltpu.VMEM((6, 32, 512), f32),
+            pltpu.VMEM((6, 128, 512), f32),
+            pltpu.VMEM((6, 128, 512), f32),
             pltpu.VMEM((6, 2, 512, 512), bf16),
             pltpu.VMEM((6, 8, 128), f32),
             pltpu.VMEM((512, 128), f32),

time: 207 us -> 203 us (0.981); the launches traced: 207 us -> 200 us
  Pallas kernels: 201 us -> 194 us
    pallas_call x1, Pallas kernels: 201 us -> 194 us  [run(): pl.pallas_call(kernel, out_shape=(jax.ShapeDtypeStruct((512, 512), f32),...]
where the time goes in v5:
time: 203 us; the launch traced here: 200 us
  Pallas kernels  194 us (96%)
  local copies, waits for them, and re-layouts  4.46 us (2%)
    pallas_call x1, Pallas kernels, run(): pl.pallas_call(kernel, out_shape=(jax.ShapeDtypeStruct((512, 512), f32),...  194 us

profile of v5, /device:TPU:1, one launch (start us, length us, event | category | flops | bytes accessed | tf_op | source)
XLA Modules:
  0.0 200.1 jit_solution(13020639758811987011)
XLA Ops:
  1.3 194.4 %shard_map.59 = (f32[512,512]{1,0:T(8,128)}, f32[8,128]{1,0:T(8,128)}) custom-call(bf16[512,512]{1,0:T(8,128)(2,1)} %fit_ref.1, bf16[512,512]{1,0:T(8,128)(2,1)} %bitcast.6, f32[1,1]{1,0:T(1,128)} %bitcast.4.occ_ref, f32[1,512]{1,0:T(1,128)} %bitcast.7), custom_call_target="tpu_custom_call" | custom-call | tf_op jit(solution)/shard_map/pallas_call | solution.py:528
  195.6 3.3 %copy.6 = f32[512,1,512]{2,1,0:T(1,128)} copy(f32[512,1,512]{2,0,1:T(8,128)} %bitcast.5) | data formatting | bytes 2097152
  198.9 1.2 slice.3

commit v6 on v5

--- a/solution.py
+++ b/solution.py
@@ -67,33 +67,33 @@
 )
 LOW_FIRST = (2, 4)
 PLAN = (
-    ("oy", 0), ("oz", 0), ("oy", 2), ("jo",), ("oy", 3), ("oy", 1), ("jl", 0), ("jl", 1), ("oz", 1),
-    ("oz", 2), ("a3", 0), ("jr", 0, 0), ("b", 0, 3), ("jr", 1, 0), ("oz", 3), ("b", 0, 1),
-    ("jg", 0), ("b", 3, 0), ("a1", 1), ("b", 0, 0), ("a1", 0), ("jg", 1), ("a3", 1), ("a1", 3),
-    ("jr", 0, 1), ("jt", 0), ("a3", 2), ("jr", 1, 1), ("a2", 0), ("b", 1, 1), ("b", 1, 0),
-    ("jt", 1), ("b", 2, 0), ("b", 3, 1), ("a1", 2), ("f1", 0), ("a2", 1), ("f2", 0), ("a2", 2),
-    ("b", 2, 1), ("b", 0, 2), ("a3", 3), ("b", 3, 2), ("b", 1, 2), ("f1", 1), ("b", 2, 2),
-    ("f2", 1), ("a2", 3), ("b", 1, 3), ("f1", 2), ("b", 3, 3), ("f2", 2), ("b", 2, 3), ("py", 0),
-    ("g", 4, 0, 1), ("py", 1), ("py", 2), ("g", 4, 0, 0), ("g", 4, 0, 2), ("g", "V", 0, 3),
-    ("f1", 3), ("g", 4, 1, 1), ("f2", 3), ("c", 1, 0), ("py", 3), ("g", "V", 1, 3), ("g", 4, 1, 0),
-    ("g", 3, 0, 0), ("c", 2, 0), ("g", 4, 2, 3), ("g", 4, 2, 0), ("g", 1, 0, 1), ("g", "N", 0, 3),
-    ("g", 3, 0, 1), ("g", 3, 1, 0), ("g", 1, 1, 0), ("g", 2, 0, 3), ("g", 3, 1, 1), ("g", 1, 1, 1),
-    ("g", 4, 2, 1), ("g", 4, 1, 2), ("c", 3, 0), ("g", 3, 0, 2), ("g", 2, 0, 2), ("g", 3, 0, 3),
-    ("c", 4, 0), ("g", "V", 2, 0), ("g", 4, 1, 3), ("g", 4, 2, 2), ("g", 4, 3, 3), ("g", 4, 3, 0),
-    ("g", 4, 3, 2), ("g", 4, 0, 3), ("g", 4, 3, 1), ("c", 1, 1), ("g", 1, 0, 3), ("g", 2, 1, 2),
-    ("g", 2, 0, 0), ("g", 3, 2, 1), ("c", 2, 1), ("g", "V", 3, 0), ("g", 1, 2, 1), ("g", 1, 2, 0),
-    ("g", 1, 1, 2), ("g", 1, 0, 0), ("g", 3, 1, 2), ("g", 3, 2, 3), ("g", 3, 3, 0), ("c", 5, 0),
-    ("g", 3, 1, 3), ("g", 2, 1, 1), ("g", 1, 2, 3), ("g", 3, 3, 3), ("g", 1, 3, 1),
-    ("g", "N", 1, 3), ("g", 1, 2, 2), ("g", 1, 0, 2), ("g", 1, 3, 0), ("g", 3, 2, 2),
-    ("g", 1, 3, 3), ("g", 1, 3, 2), ("g", 3, 2, 0), ("g", 1, 1, 3), ("c", 1, 2), ("g", 3, 3, 1),
-    ("g", 3, 3, 2), ("c", 1, 3), ("c", 3, 1), ("c", 2, 2), ("g", 2, 1, 3), ("c", 2, 3),
-    ("g", 2, 3, 1), ("g", 2, 2, 2), ("c", 4, 1), ("g", "N", 2, 0), ("g", 2, 2, 1), ("g", 2, 2, 0),
-    ("g", 2, 0, 1), ("g", "N", 3, 0), ("g", 2, 3, 0), ("g", 2, 2, 3), ("c", 3, 2), ("g", 2, 3, 2),
-    ("g", 2, 3, 3), ("g", 2, 1, 0), ("c", 1, 4), ("c", 5, 1), ("c", 3, 3), ("c", 2, 4), ("c", 4, 2),
-    ("c", 4, 3), ("c", 1, 5), ("c", 3, 4), ("c", 2, 5), ("c", 6, 1), ("c", 6, 0), ("c", 5, 2),
-    ("c", 4, 4), ("c", 5, 3), ("c", 7, 1), ("c", 6, 2), ("c", 3, 5), ("c", 4, 5), ("c", 5, 4),
-    ("c", 5, 5), ("c", 7, 2), ("c", 6, 3), ("c", 7, 0), ("c", 6, 4), ("c", 7, 3), ("c", 6, 5),
-    ("c", 7, 4), ("c", 7, 5),
+    ("oy", 2), ("oy", 1), ("oz", 0), ("oy", 0), ("jo",), ("jl", 0), ("jl", 1), ("oz", 1), ("oy", 3),
+    ("jr", 0, 0), ("oz", 2), ("a3", 0), ("a1", 0), ("jg", 0), ("oz", 3), ("a1", 1), ("b", 0, 0),
+    ("b", 0, 1), ("b", 0, 3), ("b", 3, 0), ("jt", 0), ("jg", 1), ("b", 1, 1), ("a3", 1), ("a1", 3),
+    ("jr", 0, 1), ("a3", 2), ("jr", 1, 1), ("jr", 1, 0), ("a2", 0), ("b", 3, 1), ("b", 1, 0),
+    ("jt", 1), ("b", 2, 0), ("b", 0, 2), ("a1", 2), ("f1", 0), ("a2", 1), ("f2", 0), ("a2", 2),
+    ("b", 2, 1), ("a3", 3), ("b", 3, 2), ("b", 1, 2), ("f1", 1), ("f2", 1), ("a2", 3), ("b", 2, 2),
+    ("b", 1, 3), ("py", 0), ("b", 3, 3), ("f1", 2), ("g", 4, 0, 1), ("b", 2, 3), ("py", 1),
+    ("g", 4, 0, 0), ("f2", 2), ("g", 4, 0, 2), ("g", "V", 0, 3), ("f1", 3), ("g", 4, 1, 1),
+    ("g", 3, 0, 2), ("g", 4, 1, 0), ("f2", 3), ("py", 2), ("g", "V", 1, 3), ("g", 3, 0, 0),
+    ("g", 1, 0, 2), ("g", 3, 0, 1), ("c", 1, 0), ("g", 4, 1, 3), ("py", 3), ("g", 3, 1, 0),
+    ("g", 4, 1, 2), ("g", 1, 0, 0), ("g", 3, 1, 1), ("c", 2, 0), ("g", 2, 0, 3), ("g", "V", 2, 0),
+    ("g", 4, 2, 2), ("g", 4, 2, 1), ("g", 4, 0, 3), ("g", 4, 2, 3), ("g", 3, 1, 2), ("g", 1, 2, 0),
+    ("g", "N", 0, 3), ("g", 1, 0, 1), ("g", 4, 2, 0), ("g", 1, 1, 1), ("g", 2, 1, 2),
+    ("g", 3, 0, 3), ("g", 1, 2, 1), ("c", 3, 0), ("g", 4, 3, 3), ("g", 4, 3, 0), ("g", 4, 3, 1),
+    ("g", 1, 2, 2), ("g", 4, 3, 2), ("c", 1, 1), ("c", 2, 1), ("g", 1, 3, 0), ("g", 1, 3, 1),
+    ("g", 3, 2, 1), ("g", 1, 1, 2), ("g", 1, 1, 3), ("g", 1, 3, 2), ("g", 1, 2, 3), ("g", 3, 3, 0),
+    ("g", 3, 2, 0), ("g", 3, 2, 2), ("g", 1, 0, 3), ("c", 4, 0), ("g", 3, 1, 3), ("g", 1, 3, 3),
+    ("g", 1, 1, 0), ("c", 1, 2), ("g", "N", 1, 3), ("g", 3, 3, 3), ("g", 3, 3, 2), ("g", 3, 2, 3),
+    ("g", 2, 0, 0), ("g", 2, 1, 3), ("g", 2, 0, 2), ("c", 5, 0), ("g", 3, 3, 1), ("g", 2, 1, 1),
+    ("c", 2, 2), ("g", "V", 3, 0), ("c", 1, 3), ("c", 2, 3), ("c", 3, 1), ("g", 2, 0, 1),
+    ("g", 2, 2, 3), ("c", 3, 2), ("g", 2, 2, 2), ("g", 2, 2, 0), ("c", 6, 0), ("c", 4, 1),
+    ("g", 2, 2, 1), ("g", 2, 3, 2), ("g", "N", 2, 0), ("g", 2, 3, 0), ("g", 2, 3, 3),
+    ("g", 2, 1, 0), ("g", 2, 3, 1), ("c", 1, 4), ("g", "N", 3, 0), ("c", 2, 4), ("c", 5, 1),
+    ("c", 4, 2), ("c", 3, 3), ("c", 1, 5), ("c", 3, 4), ("c", 4, 3), ("c", 2, 5), ("c", 5, 2),
+    ("c", 6, 1), ("c", 4, 4), ("c", 7, 1), ("c", 6, 2), ("c", 3, 5), ("c", 5, 3), ("c", 4, 5),
+    ("c", 5, 4), ("c", 5, 5), ("c", 7, 2), ("c", 6, 3), ("c", 7, 0), ("c", 6, 4), ("c", 7, 3),
+    ("c", 6, 5), ("c", 7, 4), ("c", 7, 5),
 )
 
 
@@ -529,7 +529,7 @@
         kernel,
         out_shape=(
             jax.ShapeDtypeStruct((512, 512), f32),
-            jax.ShapeDtypeStruct((8, 128), f32),
+            jax.ShapeDtypeStruct((1, STOPS), f32),
         ),
         in_specs=[pl.BlockSpec(memory_space=pltpu.VMEM)] * 4,
         out_specs=[pl.BlockSpec(memory_space=pltpu.VMEM)] * 2,
@@ -570,7 +570,7 @@
 
 def body(integrals, fitting, occ_energy, vir_energy):
     density, energies = run(fitting, integrals[:, 0, :], occ_energy[:, None], vir_energy[None, :])
-    return (density[:, None, :], energies[0:1, 0:STOPS])
+    return (density[:, None, :], energies)
 
 
 def solution(mesh):

time: 203 us -> 198 us (0.975); the launches traced: 200 us -> 197 us
    pallas_call x1, Pallas kernels: 194 us -> 192 us  [run(): pl.pallas_call(kernel, out_shape=(jax.ShapeDtypeStruct((512, 512), f32),...]
where the time goes in v6:
time: 198 us; the launch traced here: 197 us
  Pallas kernels  192 us (97%)
  local copies, waits for them, and re-layouts  3.79 us (2%)
    pallas_call x1, Pallas kernels, run(): pl.pallas_call(kernel, out_shape=(jax.ShapeDtypeStruct((512, 512), f32),...  192 us

profile of v6, /device:TPU:1, one launch (start us, length us, event | category | flops | bytes accessed | tf_op | source)
XLA Modules:
  0.0 197.1 jit_solution(17281576120887043802)
XLA Ops:
  1.3 192.1 %shard_map.59 = (f32[512,512]{1,0:T(8,128)}, f32[1,6]{1,0:T(1,128)}) custom-call(bf16[512,512]{1,0:T(8,128)(2,1)} %fit_ref.1, bf16[512,512]{1,0:T(8,128)(2,1)} %bitcast.6, f32[1,1]{1,0:T(1,128)} %bitcast.4.occ_ref, f32[1,512]{1,0:T(1,128)} %bitcast.7), custom_call_target="tpu_custom_call" | custom-call | tf_op jit(solution)/shard_map/pallas_call | solution.py:528
  193.3 0.0 copy-start
  193.4 3.3 %copy.6 = f32[512,1,512]{2,1,0:T(1,128)} copy(f32[512,1,512]{2,0,1:T(8,128)} %bitcast.5) | data formatting | bytes 2097152
  196.6 0.0 copy-done
  196.6 0.5 copy.9
Async XLA Ops:
  193.3 3.3 %copy-start = (f32[1,6]{1,0:T(1,128)S(1)}, f32[1,6]{1,0:T(1,128)}, u32[]{:S(2)}) copy-start(f32[1,6]{1,0:T(1,128)} %get-tuple-element.11) | copy-start | bytes 76

commit v7 on v6

--- a/solution.py
+++ b/solution.py
@@ -130,7 +130,7 @@
 
 def kernel(
     fit_ref, int_ref, occ_ref, vir_ref, out_ref, en_ref,
-    fb, ib, acc, pt, spare, ownt, pbo, hb, cb, xb, qb, zb, qz, zz, am, eb, vcol,
+    fb, ib, acc, pt, spare, ownt, pbo, hb, cb, xb, qb, zb, qz, zz, am, eb, vcol, dens,
     fs, fr, js, jr, rs, rr, es, er, cs, cr, xs, xr, zs, zr, azs, azr, axs, axr, acs, acr,
 ):
     at = Place()
@@ -436,7 +436,7 @@
         for n in range(ac_parts(k)):
             ac_copy(k, n).wait_recv()
         hi, lo = pt[k, 0], pt[k, 1]
-        out_ref[...] += dot_nt(hi, am[k, 0]) + dot_nt(hi, am[k, 1]) + dot_nt(lo, am[k, 0])
+        dens[...] += dot_nt(hi, am[k, 0]) + dot_nt(hi, am[k, 1]) + dot_nt(lo, am[k, 0])
         energy = eb[0, 0:1, 0:1] + eb[k, 0:1, 0:1]
         total = jnp.zeros((1, 1), jnp.float32)
         for r in range(4):
@@ -452,7 +452,7 @@
         fb[at.occ] = fit_ref[...]
         ib[at.fit] = int_ref[...]
         eb[0] = jnp.broadcast_to(occ_ref[...], (8, 128))
-        out_ref[...] = jnp.zeros_like(out_ref)
+        dens[...] = jnp.zeros_like(dens)
         en_ref[...] = jnp.zeros_like(en_ref)
         vcol[...] = jnp.broadcast_to(vir_ref[...], (128, 512)).T
         for d in range(1, 6):
@@ -501,6 +501,7 @@
                 energy_copy(d).wait_recv()
         steps[name](*rest)
 
+    out_ref[:, 0, :] = dens[...]
     for n in range(20):
         lax.fori_loop(0, CHUNKS, lambda c, _: (f_copy(n, c).wait_send(), _)[1], 0)
     for n in range(len(HOPS)):
@@ -528,7 +529,7 @@
     return pl.pallas_call(
         kernel,
         out_shape=(
-            jax.ShapeDtypeStruct((512, 512), f32),
+            jax.ShapeDtypeStruct((512, 1, 512), f32),
             jax.ShapeDtypeStruct((1, STOPS), f32),
         ),
         in_specs=[pl.BlockSpec(memory_space=pltpu.VMEM)] * 4,
@@ -551,6 +552,7 @@
             pltpu.VMEM((6, 2, 512, 512), bf16),
             pltpu.VMEM((6, 8, 128), f32),
             pltpu.VMEM((512, 128), f32),
+            pltpu.VMEM((512, 512), f32),
             dma((20, CHUNKS)), dma((16, CHUNKS, 2)),
             dma((len(HOPS),)), dma((16, 2)),
             dma((len(ROUTES), CHUNKS)), dma((8, CHUNKS)),
@@ -570,7 +572,7 @@
 
 def body(integrals, fitting, occ_energy, vir_energy):
     density, energies = run(fitting, integrals[:, 0, :], occ_energy[:, None], vir_energy[None, :])
-    return (density[:, None, :], energies)
+    return (density, energies)
 
 
 def solution(mesh):

time: 198 us -> 198 us (level)
  no operation moved by 1% of the time
where the time goes in v7:
time: 198 us; the launch traced here: 197 us
  Pallas kernels  192 us (97%)
  local copies, waits for them, and re-layouts  3.43 us (2%)
    pallas_call x1, Pallas kernels, run(): pl.pallas_call(kernel, out_shape=(jax.ShapeDtypeStruct((512, 1, 512), f32...  192 us

profile of v7, /device:TPU:1, one launch (start us, length us, event | category | flops | bytes accessed | tf_op | source)
XLA Modules:
  0.0 196.7 jit_solution(14086909451601873305)
XLA Ops:
  1.3 191.9 %shard_map.59 = (f32[512,1,512]{2,1,0:T(1,128)}, f32[1,6]{1,0:T(1,128)}) custom-call(bf16[512,512]{1,0:T(8,128)(2,1)} %fit_ref.1, bf16[512,512]{1,0:T(8,128)(2,1)} %bitcast.4, f32[1,1]{1,0:T(1,128)} %bitcast.3.occ_ref, f32[1,512]{1,0:T(1,128)} %bitcast.5), custom_call_target="tpu_custom_call" | custom-call | tf_op jit(solution)/shard_map/pallas_call | solution.py:529
  193.2 0.0 copy-start
  193.2 2.9 %copy.9 = f32[512,1,512]{2,1,0:T(1,128)} copy(f32[512,1,512]{2,1,0:T(1,128)} %get-tuple-element.4) | data formatting | bytes 2097152
  196.2 0.0 copy-done
  196.2 0.5 copy.10
Async XLA Ops:
  193.2 2.9 %copy-start = (f32[1,6]{1,0:T(1,128)S(1)}, f32[1,6]{1,0:T(1,128)}, u32[]{:S(2)}) copy-start(f32[1,6]{1,0:T(1,128)} %get-tuple-element.5) | copy-start | bytes 76
